TPU v7x, 32 devices: a whole 2x2x4 slice. The times are simulated.
32 devices in a mesh: ax: 8 (over z, y), rad: 4 (over x, core).
Axes of the slice: x: 2, y: 2, z: 4, core: 2. Of those that a mesh axis runs over, the one named last changes fastest.
Arguments:
- face_data: float32 [1024, 7, 5, 128], P('ax', None, None, 'rad'), may hold values from -0.6 to 0.6
- face_station: int32 [1024], P('ax'), may hold values from 0 to 511, as said below
- face_counts: int32 [8], P('ax'), may hold values from 0 to 128, as said below
- mode_slots: int32 [256], replicated, may hold values from 0 to 255, each once
- radial_proj: float32 [32, 128], P(None, 'rad'), may hold values from -0.5 to 0.5
- radial_modes: float32 [64, 32], replicated, may hold values from -1 to 1
- duct_field: float32 [32, 64, 3, 5, 2, 256], P('ax', 'rad'), may hold values from -6 to 6
- mean_mach: float32 [32, 64], P('ax', 'rad'), may hold values from 0.1 to 0.7
- pseudo_step: float32 [32, 64], P('ax', 'rad'), may hold values from 0.06 to 0.2
Outputs:
- duct_next: float32 [32, 64, 3, 5, 2, 256], P('ax', 'rad')
Inputs may be any that keep to these rules, and one draw needn't show every extreme that they name: `face_counts`: they sum to 512; one index of ax uses all 128 slots. `face_station`: slot s of ax index a is used when s < face_counts[a] and then names an angular station; each station is named by exactly one used slot; unused slots name arbitrary stations. `mode_slots`: each circumferential mode once.
All inputs are finite; a program needn't handle non-finite values.
Results may differ from a plain program's by a relative error of at most 0.00012.
Values sent between devices are 32-bit elements; how exact they have to be, the bound alone decides.
A program may use at most 128 MiB of HBM per device.

v0:
```python
import math

import jax
import jax.numpy as jnp
from jax import lax
from jax.sharding import PartitionSpec as P

NTH = 512
SAMPLE_MOMENTS = 7
HARM = 3
NMODE = 256
NRD = 64
ITERS = 3


OMEGA_STEP = 0.35
DAMPING = 0.25


def extended(cells, sides, width):
    for axis, dim in sides:
        count = lax.axis_size(axis)
        ends = count - 1
        head = lax.slice_in_dim(cells, 0, width, axis=dim)
        tail = lax.slice_in_dim(cells, cells.shape[dim] - width, cells.shape[dim], axis=dim)
        cells = jnp.concatenate(
            [
                lax.ppermute(tail, axis, [(i, (i + 1) % count) for i in range(ends)]),
                cells,
                lax.ppermute(head, axis, [((i + 1) % count, i) for i in range(ends)]),
            ],
            axis=dim,
        )
    return cells


def rotate(part):
    return jnp.stack([-part[..., 1, :], part[..., 0, :]], axis=-2)


def advance(padded, mach, step_size, inv_radius, modes):
    centre = padded[1:-1, 1:-1]
    along = (padded[2:, 1:-1] - padded[:-2, 1:-1]) * 0.5
    across = (padded[1:-1, 2:] - padded[1:-1, :-2]) * 0.5
    damped_filter = (
        padded[2:, 1:-1] + padded[:-2, 1:-1] + padded[1:-1, 2:] + padded[1:-1, :-2] - 4.0 * centre
    )
    frequency_order = jnp.arange(1, HARM + 1).astype(jnp.float32)
    omega = (OMEGA_STEP * frequency_order)[:, None, None]
    mach_cell = mach[:, :, None, None, None]
    radius_cell = inv_radius[None, :, None, None, None]
    density = centre[:, :, :, 0]
    axial = centre[:, :, :, 1]
    radial = centre[:, :, :, 2]
    swirl = centre[:, :, :, 3]
    pressure = centre[:, :, :, 4]
    source = (
        along[:, :, :, 1]
        + across[:, :, :, 2]
        + radial * radius_cell
        + rotate(swirl) * modes * radius_cell
    )
    res_density = omega * rotate(density) + mach_cell * along[:, :, :, 0] + source
    res_axial = omega * rotate(axial) + mach_cell * along[:, :, :, 1] + along[:, :, :, 4]
    res_radial = omega * rotate(radial) + mach_cell * along[:, :, :, 2] + across[:, :, :, 4]
    res_swirl = (
        omega * rotate(swirl)
        + mach_cell * along[:, :, :, 3]
        + rotate(pressure) * modes * radius_cell
    )
    res_pressure = omega * rotate(pressure) + mach_cell * along[:, :, :, 4] + source
    residual = jnp.stack([res_density, res_axial, res_radial, res_swirl, res_pressure], axis=3)
    step_cell = step_size[:, :, None, None, None, None]
    return centre - step_cell * (residual - DAMPING * damped_filter)


def project(face_data, face_station, valid, wave_orders, radial_proj):
    frequency_order = jnp.arange(1, HARM + 1)
    sample_moments = jnp.arange(SAMPLE_MOMENTS)
    revolution_count = (frequency_order[:, None] * sample_moments[None, :] % SAMPLE_MOMENTS).astype(
        jnp.float32
    ) * (2.0 * math.pi / SAMPLE_MOMENTS)
    twiddle = jnp.stack([jnp.cos(revolution_count), -jnp.sin(revolution_count)], axis=1) * (
        2.0 / SAMPLE_MOMENTS
    )
    spectral_values = jnp.einsum(
        "rtvj,kct->rkvcj", face_data, twiddle, precision=lax.Precision.HIGHEST
    )
    phase = jnp.mod(face_station[:, None] * wave_orders[None, :], NTH).astype(jnp.float32) * (
        2.0 * math.pi / NTH
    )
    cosine = jnp.where(valid[:, None], jnp.cos(phase), 0.0)
    sine = jnp.where(valid[:, None], jnp.sin(phase), 0.0)
    with_cos = jnp.einsum(
        "rs,rkvcj->kvcjs", cosine, spectral_values, precision=lax.Precision.HIGHEST
    )
    with_sin = jnp.einsum("rs,rkvcj->kvcjs", sine, spectral_values, precision=lax.Precision.HIGHEST)
    real_part = with_cos[:, :, 0] + with_sin[:, :, 1]
    imag_part = with_cos[:, :, 1] - with_sin[:, :, 0]
    fourier_transform = jnp.stack([real_part, imag_part], axis=2)
    return jnp.einsum(
        "nj,kvcjs->nkvcs", radial_proj, fourier_transform, precision=lax.Precision.HIGHEST
    )


def on_device(
    face_data,
    face_station,
    face_counts,
    mode_slots,
    radial_proj,
    radial_modes,
    duct_field,
    mean_mach,
    pseudo_step,
):
    slot_ids = jnp.arange(face_station.shape[0])
    valid = slot_ids < face_counts[0]
    wave_orders = mode_slots - NMODE // 2
    partial_value = project(face_data, face_station, valid, wave_orders, radial_proj)
    rows_here = duct_field.shape[1]
    radial_index = lax.axis_index("rad")
    totals = lax.psum(partial_value, ("ax", "rad"))
    shape_rows = lax.dynamic_slice_in_dim(radial_modes, radial_index * rows_here, rows_here, 0)
    boundary = jnp.einsum("jn,nkvcs->jkvcs", shape_rows, totals, precision=lax.Precision.HIGHEST)
    modes = wave_orders.astype(jnp.float32)
    radial_start = radial_index * rows_here
    global_rows = (radial_start + jnp.arange(rows_here)).astype(jnp.float32)
    inv_radius = 1.0 / (NRD + global_rows + 0.5)
    at_inlet = lax.axis_index("ax") == 0
    field = duct_field
    for sweep in range(ITERS):
        padded = extended(field, (("ax", 0), ("rad", 1)), 1)
        ghost = jnp.where(at_inlet, boundary, padded[0, 1:-1])
        padded = padded.at[0, 1:-1].set(ghost)
        field = advance(padded, mean_mach, pseudo_step, inv_radius, modes)
    return field


def solution(mesh):
    in_specs = (
        P("ax", None, None, "rad"),
        P("ax"),
        P("ax"),
        P(),
        P(None, "rad"),
        P(),
        P("ax", "rad", None, None, None, None),
        P("ax", "rad"),
        P("ax", "rad"),
    )
    out_specs = P("ax", "rad", None, None, None, None)
    return jax.shard_map(
        on_device, mesh=mesh, in_specs=in_specs, out_specs=out_specs, check_vma=False
    )
```

profile of v0, /device:TPU:1, one launch (start us, length us, event | category | flops | bytes accessed | tf_op | source)
XLA Modules:
  0.0 294.7 jit_solution(11995770886220923457)
XLA Ops:
  6.5 1.2 slice.457
  7.8 4.1 %collective-permute-start = (f32[1,16,3,5,2,256]{5,1,2,4,3,0:T(8,128)S(1)}, f32[1,16,3,5,2,256]{5,1,2,4,3,0:T(8,128)S(1)}, u32[]{:S(2)}, u32[]{:S(2)}) collective-permute-start(f32[1,16,3,5,2,256]{5,1,2,4,3,0:T(8,128)S(1)} %copy.42), channel_id=1, source_target_pairs={{0,4},{4,8},{8,12},{12,16},{16,20},{20,24},{24,28},{1,5},{5,9},{9,... | collective-permute-start | bytes 1474568 | tf_op jit(solution)/shard_map/ppermute | solution.py:28
  12.0 1.8 copy.13
  13.8 0.8 slice.556
  14.7 1.3 collective-permute-start.1
  16.8 1.2 convolution_bitcast_fusion.1
  18.0 1.5 fusion.47
  19.5 1.5 fusion.49
  21.0 0.2 slice_add_fusion
  21.2 1.9 convolution_bitcast_fusion
  23.1 0.7 fusion.118
  23.8 9.2 %collective-permute-done = f32[1,16,3,5,2,256]{5,1,2,4,3,0:T(8,128)S(1)} collective-permute-done((f32[1,16,3,5,2,256]{5,1,2,4,3,0:T(8,128)S(1)}, f32[1,16,3,5,2,256]{5,1,2,4,3,0:T(8,128)S(1)}, u32[]{:S(2)}, u32[]{:S(2)}) %collective-permute-start) | collective-permute-done | bytes 491552 | tf_op jit(solution)/shard_map/ppermute | solution.py:28
  33.0 1.0 pad_maximum_fusion.17
  34.0 4.5 %collective-permute-start.2 = (f32[6,1,3,5,2,256]{5,1,2,0,4,3:T(1,128)}, f32[6,1,3,5,2,256]{5,1,2,0,4,3:T(1,128)}, u32[]{:S(2)}, u32[]{:S(2)}) collective-permute-start(f32[6,1,3,5,2,256]{5,1,2,0,4,3:T(1,128)} %get-tuple-element.76), channel_id=1, source_target_pairs={{0,1},{1,2},{2,3},{4,5},{5,6},{6,7},{8,9},{9,10},{10,11},{12,13},{... | collective-permute-start | bytes 552968 | tf_op jit(solution)/shard_map/ppermute | solution.py:28
  38.5 1.9 collective-permute-start.3
  40.5 115.2 %all-reduce.2.cloned.1.call-done = f32[32,3,5,2,256]{4,0,3,2,1:T(8,128)} async-done(((f32[32,3,5,2,256]{4,0,3,2,1:T(8,128)}), f32[32,3,5,2,256]{4,0,3,2,1:T(8,128)}) %all-reduce.2.cloned.1.call-update) | async-done | bytes 983056 | tf_op jit(solution)/shard_map/psum | solution.py:123
  155.6 1.9 fusion.82
  157.5 0.9 fusion.7
  158.4 3.8 %pad_maximum_fusion = f32[6,18,3,5,2,256]{5,1,2,0,4,3:T(8,128)} fusion(f32[6,1,3,5,2,256]{5,1,2,0,4,3:T(1,128)} %collective-permute-done.3, f32[1,16,3,5,2,256]{5,1,2,0,4,3:T(8,128)S(1)} %collective-permute-done.1, f32[4,16,3,5,2,256]{5,1,2,0,4,3:T(8,128)S(1)} %copy.13, f32[1,16,3,5,2,256]{5,1,2,0,4,3:T(8,128)S(1)} %bitcast.166, ...), kind=kLoop, calls=%fused_computation | loop fusion | flops 3317760 | bytes 6635520 | tf_op jit(solution)/shard_map/concatenate | solution.py:26
  162.2 5.0 %scatter.10 = f32[6,18,3,5,2,256]{5,1,2,0,4,3:T(8,128)} dynamic-update-slice(f32[6,18,3,5,2,256]{5,1,2,0,4,3:T(8,128)} %pad_maximum_fusion, f32[1,16,3,5,2,256]{5,1,2,0,4,3:T(8,128)} %fusion.7, s32[]{:T(128)} %bitcast.17, s32[]{:T(128)} %bitcast.18, s32[]{:T(128)} %constant.117.clone.1, s32[]{:T(128)} %constant.117.clone.1, s32[]{:T(128)} %constant.117.clone.1, s32[]{:T(128)} %constant.117.clone.1) | dynamic-update-slice | bytes 983044 | tf_op jit(solution)/shard_map/scatter | solution.py:135
  167.2 2.3 slice_bitcast_fusion.6
  169.5 5.5 %subtract_multiply_fusion.5 = (f32[4,16,3,5,2,256]{5,1,2,0,4,3:T(8,128)S(1)}, f32[4,16,3,5,2,256]{5,1,2,0,4,3:T(8,128)S(1)}) fusion(f32[6,18,3,5,2,256]{5,1,2,0,4,3:T(8,128)} %scatter.10), kind=kLoop, calls=%fused_computation.11 | loop fusion | flops 1966080 | bytes 11796480 | tf_op jit(solution)/shard_map/mul | solution.py:44
  175.2 0.4 copy-done.8
  175.7 0.3 fusion.37
  176.3 0.2 fusion.30
  176.6 0.4 copy-done.9
  177.0 1.0 multiply_subtract_fusion.1
  178.0 3.3 %collective-permute-start.4 = (f32[1,16,3,5,2,256]{5,1,2,4,3,0:T(8,128)S(1)}, f32[1,16,3,5,2,256]{5,1,2,4,3,0:T(8,128)S(1)}, u32[]{:S(2)}, u32[]{:S(2)}) collective-permute-start(f32[1,16,3,5,2,256]{5,1,2,4,3,0:T(8,128)S(1)} %get-tuple-element.80), channel_id=1, source_target_pairs={{0,4},{4,8},{8,12},{12,16},{16,20},{20,24},{24,28},{1,5},{5,9},{9,... | collective-permute-start | bytes 1474568 | tf_op jit(solution)/shard_map/ppermute | solution.py:28
  181.3 1.3 collective-permute-start.5
  182.6 19.3 %collective-permute-done.4 = f32[1,16,3,5,2,256]{5,1,2,4,3,0:T(8,128)S(1)} collective-permute-done((f32[1,16,3,5,2,256]{5,1,2,4,3,0:T(8,128)S(1)}, f32[1,16,3,5,2,256]{5,1,2,4,3,0:T(8,128)S(1)}, u32[]{:S(2)}, u32[]{:S(2)}) %collective-permute-start.4) | collective-permute-done | bytes 491552 | tf_op jit(solution)/shard_map/ppermute | solution.py:28
  202.0 0.3 pad_maximum_fusion.14
  202.2 3.4 %collective-permute-start.6 = (f32[6,1,3,5,2,256]{5,1,2,0,4,3:T(1,128)S(1)}, f32[6,1,3,5,2,256]{5,1,2,0,4,3:T(1,128)S(1)}, u32[]{:S(2)}, u32[]{:S(2)}) collective-permute-start(f32[6,1,3,5,2,256]{5,1,2,0,4,3:T(1,128)S(1)} %get-tuple-element.74), channel_id=1, source_target_pairs={{0,1},{1,2},{2,3},{4,5},{5,6},{6,7},{8,9},{9,10},{10,11},{12,13},{... | collective-permute-start | bytes 552968 | tf_op jit(solution)/shard_map/ppermute | solution.py:28
  205.6 1.9 collective-permute-start.7
  207.6 0.4 collective-permute-done.6
  208.1 4.4 %collective-permute-done.7 = f32[6,1,3,5,2,256]{5,1,2,0,4,3:T(1,128)S(1)} collective-permute-done((f32[6,1,3,5,2,256]{5,1,2,0,4,3:T(1,128)S(1)}, f32[6,1,3,5,2,256]{5,1,2,0,4,3:T(1,128)S(1)}, u32[]{:S(2)}, u32[]{:S(2)}) %collective-permute-start.7) | collective-permute-done | bytes 184352 | tf_op jit(solution)/shard_map/ppermute | solution.py:30
  212.5 2.9 pad_maximum_fusion.1
  215.3 4.9 %scatter.11 = f32[6,18,3,5,2,256]{5,1,2,0,4,3:T(8,128)} dynamic-update-slice(f32[6,18,3,5,2,256]{5,1,2,0,4,3:T(8,128)} %pad_maximum_fusion.1, f32[1,16,3,5,2,256]{5,1,2,0,4,3:T(8,128)S(1)} %fusion.6, s32[]{:T(128)} %bitcast.17, s32[]{:T(128)} %bitcast.18, s32[]{:T(128)} %constant.117.clone.1, s32[]{:T(128)} %constant.117.clone.1, s32[]{:T(128)} %constant.117.clone.1, s32[]{:T(128)} %constant.117.clone.1) | dynamic-update-slice | bytes 983044 | tf_op jit(solution)/shard_map/scatter | solution.py:135
  220.2 2.2 slice_bitcast_fusion.2
  222.4 6.6 %fusion.116 = (f32[4,16,3,5,2,256]{5,1,2,0,4,3:T(8,128)S(1)}, f32[4,16,3,5,2,256]{5,1,2,0,4,3:T(8,128)S(1)}, f32[4,16,3,5,2,256]{5,1,2,0,4,3:T(8,128)S(1)}) fusion(f32[6,18,3,5,2,256]{5,1,2,0,4,3:T(8,128)} %scatter.11), kind=kLoop, calls=%fused_computation.232 | loop fusion | flops 1966080 | bytes 15728640 | tf_op jit(solution)/shard_map/slice | solution.py:42
  229.3 0.3 fusion.27
  229.9 0.2 fusion.20
  230.2 1.0 copy_subtract_fusion
  231.3 4.1 %collective-permute-start.8 = (f32[1,16,3,5,2,256]{5,1,4,3,2,0:T(8,128)S(1)}, f32[1,16,3,5,2,256]{5,1,4,3,2,0:T(8,128)S(1)}, u32[]{:S(2)}, u32[]{:S(2)}) collective-permute-start(f32[1,16,3,5,2,256]{5,1,4,3,2,0:T(8,128)S(1)} %get-tuple-element.78), channel_id=1, source_target_pairs={{0,4},{4,8},{8,12},{12,16},{16,20},{20,24},{24,28},{1,5},{5,9},{9,... | collective-permute-start | bytes 1474568 | tf_op jit(solution)/shard_map/ppermute | solution.py:28
  235.4 1.3 collective-permute-start.9
  236.7 17.2 %collective-permute-done.8 = f32[1,16,3,5,2,256]{5,1,4,3,2,0:T(8,128)S(1)} collective-permute-done((f32[1,16,3,5,2,256]{5,1,4,3,2,0:T(8,128)S(1)}, f32[1,16,3,5,2,256]{5,1,4,3,2,0:T(8,128)S(1)}, u32[]{:S(2)}, u32[]{:S(2)}) %collective-permute-start.8) | collective-permute-done | bytes 491552 | tf_op jit(solution)/shard_map/ppermute | solution.py:28
  253.9 0.3 pad_maximum_fusion.11
  254.1 1.9 collective-permute-start.10
  256.1 2.6 collective-permute-start.11
  258.8 4.1 %collective-permute-done.11 = f32[6,1,3,5,2,256]{5,1,4,3,2,0:T(1,128)S(1)} collective-permute-done((f32[6,1,3,5,2,256]{5,1,4,3,2,0:T(1,128)S(1)}, f32[6,1,3,5,2,256]{5,1,4,3,2,0:T(1,128)S(1)}, u32[]{:S(2)}, u32[]{:S(2)}) %collective-permute-start.11) | collective-permute-done | bytes 184352 | tf_op jit(solution)/shard_map/ppermute | solution.py:30
  262.9 2.8 pad_maximum_fusion.2
  265.8 4.9 %scatter.14 = f32[6,18,3,5,2,256]{5,1,4,3,2,0:T(8,128)} dynamic-update-slice(f32[6,18,3,5,2,256]{5,1,4,3,2,0:T(8,128)} %pad_maximum_fusion.2, f32[1,16,3,5,2,256]{5,1,4,3,2,0:T(8,128)S(1)} %fusion.5, s32[]{:T(128)} %bitcast.17, s32[]{:T(128)} %bitcast.18, s32[]{:T(128)} %constant.117.clone.1, s32[]{:T(128)} %constant.117.clone.1, s32[]{:T(128)} %constant.117.clone.1, s32[]{:T(128)} %constant.117.clone.1) | dynamic-update-slice | bytes 983044 | tf_op jit(solution)/shard_map/scatter | solution.py:135
  270.7 3.1 %slice_bitcast_fusion.1 = (f32[4,16,3,2,256]{4,1,3,2,0:T(8,128)S(1)}, f32[4,16,3,1,2,256]{5,1,4,3,2,0:T(8,128)}, f32[4,16,3,1,2,256]{5,1,4,3,2,0:T(8,128)}, f32[...) fusion(f32[6,18,3,5,2,256]{5,1,4,3,2,0:T(8,128)} %scatter.14), kind=kLoop, calls=%fused_computation.29 | loop fusion | bytes 3932160 | tf_op jit(solution)/shard_map/squeeze | solution.py:56
  273.8 2.9 fusion.115
  276.7 1.0 copy.83
  277.9 1.3 copy-done.3
  279.3 0.6 copy-done.4
  279.9 0.5 subtract_multiply_fusion.1
  280.4 0.5 subtract_multiply_fusion
  280.8 0.5 copy-done.6
  281.4 0.3 fusion.17
  282.0 0.2 fusion.10
  282.3 1.2 copy-done.5
  283.5 1.5 multiply_subtract_fusion
  285.1 2.8 copy.36
  (75 shorter events, 2.5 us)
Async XLA Ops:
  6.5 14.6 %copy-start = (f32[32,32]{1,0:T(8,128)S(1)}, f32[32,32]{1,0:T(8,128)}, u32[]{:S(2)}) copy-start(f32[32,32]{1,0:T(8,128)} %param.19) | copy-start | bytes 12292
  6.5 149.1 %all-reduce.2.cloned.1.call-start = ((), (), s32[]{:S(2)}) async-start(), calls=%async_computation | async-start | bytes 1966080 | tf_op jit(solution)/shard_map/psum | solution.py:123
  7.8 8.8 %copy-start.12 = (s32[256]{0:T(256)S(1)}, s32[256]{0:T(256)}, u32[]{:S(2)}) copy-start(s32[256]{0:T(256)} %param.18) | copy-start | bytes 3076
  7.8 8.9 %copy-start.7 = (f32[128,7,5,32]{0,3,2,1:T(8,128)S(1)}, f32[128,7,5,32]{0,3,2,1:T(8,128)}, u32[]{:S(2)}) copy-start(f32[128,7,5,32]{0,3,2,1:T(8,128)} %param.15) | copy-start | bytes 1720324
  7.8 25.2 %collective-permute-start = (f32[1,16,3,5,2,256]{5,1,2,4,3,0:T(8,128)S(1)}, f32[1,16,3,5,2,256]{5,1,2,4,3,0:T(8,128)S(1)}, u32[]{:S(2)}, u32[]{:S(2)}) collective-permute-start(f32[1,16,3,5,2,256]{5,1,2,4,3,0:T(8,128)S(1)} %copy.42), channel_id=1, source_target_pairs={{0,4},{4,8},{8,12},{12,16},{16,20},{20,24},{24,28},{1,5},{5,9},{9,... | collective-permute-start | bytes 1474568 | tf_op jit(solution)/shard_map/ppermute | solution.py:28
  13.8 4.2 %copy-start.11 = (s32[128]{0:T(128)S(1)}, s32[128]{0:T(128)}, u32[]{:S(2)}) copy-start(s32[128]{0:T(128)} %param.16) | copy-start | bytes 1540
  14.7 18.4 %collective-permute-start.1 = (f32[1,16,3,5,2,256]{5,1,2,0,4,3:T(8,128)}, f32[1,16,3,5,2,256]{5,1,2,0,4,3:T(8,128)S(1)}, u32[]{:S(2)}, u32[]{:S(2)}) collective-permute-start(f32[1,16,3,5,2,256]{5,1,2,0,4,3:T(8,128)} %slice.556), channel_id=1, source_target_pairs={{4,0},{8,4},{12,8},{16,12},{20,16},{24,20},{28,24},{5,1},{9,5},{13... | collective-permute-start | bytes 1474568 | tf_op jit(solution)/shard_map/ppermute | solution.py:30
  23.1 132.6 %copy-start.10 = (f32[64,32]{0,1:T(8,128)S(1)}, f32[64,32]{0,1:T(8,128)}, u32[]{:S(2)}) copy-start(f32[64,32]{0,1:T(8,128)} %param.20) | copy-start | bytes 24580
  34.0 124.3 %collective-permute-start.2 = (f32[6,1,3,5,2,256]{5,1,2,0,4,3:T(1,128)}, f32[6,1,3,5,2,256]{5,1,2,0,4,3:T(1,128)}, u32[]{:S(2)}, u32[]{:S(2)}) collective-permute-start(f32[6,1,3,5,2,256]{5,1,2,0,4,3:T(1,128)} %get-tuple-element.76), channel_id=1, source_target_pairs={{0,1},{1,2},{2,3},{4,5},{5,6},{6,7},{8,9},{9,10},{10,11},{12,13},{... | collective-permute-start | bytes 552968 | tf_op jit(solution)/shard_map/ppermute | solution.py:28
  38.5 119.8 %collective-permute-start.3 = (f32[6,1,3,5,2,256]{5,1,2,0,4,3:T(1,128)}, f32[6,1,3,5,2,256]{5,1,2,0,4,3:T(1,128)}, u32[]{:S(2)}, u32[]{:S(2)}) collective-permute-start(f32[6,1,3,5,2,256]{5,1,2,0,4,3:T(1,128)} %get-tuple-element.77), channel_id=1, source_target_pairs={{1,0},{2,1},{3,2},{5,4},{6,5},{7,6},{9,8},{10,9},{11,10},{13,12},{... | collective-permute-start | bytes 552968 | tf_op jit(solution)/shard_map/ppermute | solution.py:30
  167.2 8.0 %slice-start.2 = ((s8[4423680]{0:T(1024)(128)(4,1)}), s8[4194304]{0:T(1024)(128)(4,1)S(1)}, s32[]{:S(2)}) async-start(s8[4423680]{0:T(1024)(128)(4,1)} %bitcast.163), calls=%async_computation.3 | async-start | bytes 8388608
  169.5 5.7 %slice-start.3 = ((s8[4423680]{0:T(1024)(128)(4,1)}), s8[229376]{0:T(1024)(128)(4,1)S(1)}, s32[]{:S(2)}) async-start(s8[4423680]{0:T(1024)(128)(4,1)} %bitcast.163), calls=%async_computation.4 | async-start | bytes 458752
  175.0 0.7 copy-start.8
  176.3 0.7 copy-start.9
  178.0 23.9 %collective-permute-start.4 = (f32[1,16,3,5,2,256]{5,1,2,4,3,0:T(8,128)S(1)}, f32[1,16,3,5,2,256]{5,1,2,4,3,0:T(8,128)S(1)}, u32[]{:S(2)}, u32[]{:S(2)}) collective-permute-start(f32[1,16,3,5,2,256]{5,1,2,4,3,0:T(8,128)S(1)} %get-tuple-element.80), channel_id=1, source_target_pairs={{0,4},{4,8},{8,12},{12,16},{16,20},{20,24},{24,28},{1,5},{5,9},{9,... | collective-permute-start | bytes 1474568 | tf_op jit(solution)/shard_map/ppermute | solution.py:28
  181.3 20.6 %collective-permute-start.5 = (f32[1,16,3,5,2,256]{5,1,2,0,4,3:T(8,128)S(1)}, f32[1,16,3,5,2,256]{5,1,2,0,4,3:T(8,128)S(1)}, u32[]{:S(2)}, u32[]{:S(2)}) collective-permute-start(f32[1,16,3,5,2,256]{5,1,2,0,4,3:T(8,128)S(1)} %get-tuple-element.81), channel_id=1, source_target_pairs={{4,0},{8,4},{12,8},{16,12},{20,16},{24,20},{28,24},{5,1},{9,5},{13... | collective-permute-start | bytes 1474568 | tf_op jit(solution)/shard_map/ppermute | solution.py:30
  202.2 5.9 %collective-permute-start.6 = (f32[6,1,3,5,2,256]{5,1,2,0,4,3:T(1,128)S(1)}, f32[6,1,3,5,2,256]{5,1,2,0,4,3:T(1,128)S(1)}, u32[]{:S(2)}, u32[]{:S(2)}) collective-permute-start(f32[6,1,3,5,2,256]{5,1,2,0,4,3:T(1,128)S(1)} %get-tuple-element.74), channel_id=1, source_target_pairs={{0,1},{1,2},{2,3},{4,5},{5,6},{6,7},{8,9},{9,10},{10,11},{12,13},{... | collective-permute-start | bytes 552968 | tf_op jit(solution)/shard_map/ppermute | solution.py:28
  205.6 6.9 %collective-permute-start.7 = (f32[6,1,3,5,2,256]{5,1,2,0,4,3:T(1,128)S(1)}, f32[6,1,3,5,2,256]{5,1,2,0,4,3:T(1,128)S(1)}, u32[]{:S(2)}, u32[]{:S(2)}) collective-permute-start(f32[6,1,3,5,2,256]{5,1,2,0,4,3:T(1,128)S(1)} %get-tuple-element.75), channel_id=1, source_target_pairs={{1,0},{2,1},{3,2},{5,4},{6,5},{7,6},{9,8},{10,9},{11,10},{13,12},{... | collective-permute-start | bytes 552968 | tf_op jit(solution)/shard_map/ppermute | solution.py:30
  220.2 9.0 %slice-start = ((s8[4423680]{0:T(1024)(128)(4,1)}), s8[4194304]{0:T(1024)(128)(4,1)S(1)}, s32[]{:S(2)}) async-start(s8[4423680]{0:T(1024)(128)(4,1)} %bitcast.161), calls=%async_computation.1 | async-start | bytes 8388608
  222.4 6.8 %slice-start.1 = ((s8[4423680]{0:T(1024)(128)(4,1)}), s8[229376]{0:T(1024)(128)(4,1)S(1)}, s32[]{:S(2)}) async-start(s8[4423680]{0:T(1024)(128)(4,1)} %bitcast.161), calls=%async_computation.2 | async-start | bytes 458752
  231.3 22.6 %collective-permute-start.8 = (f32[1,16,3,5,2,256]{5,1,4,3,2,0:T(8,128)S(1)}, f32[1,16,3,5,2,256]{5,1,4,3,2,0:T(8,128)S(1)}, u32[]{:S(2)}, u32[]{:S(2)}) collective-permute-start(f32[1,16,3,5,2,256]{5,1,4,3,2,0:T(8,128)S(1)} %get-tuple-element.78), channel_id=1, source_target_pairs={{0,4},{4,8},{8,12},{12,16},{16,20},{20,24},{24,28},{1,5},{5,9},{9,... | collective-permute-start | bytes 1474568 | tf_op jit(solution)/shard_map/ppermute | solution.py:28
  235.4 18.5 %collective-permute-start.9 = (f32[1,16,3,5,2,256]{5,1,4,3,2,0:T(8,128)S(1)}, f32[1,16,3,5,2,256]{5,1,4,3,2,0:T(8,128)S(1)}, u32[]{:S(2)}, u32[]{:S(2)}) collective-permute-start(f32[1,16,3,5,2,256]{5,1,4,3,2,0:T(8,128)S(1)} %get-tuple-element.79), channel_id=1, source_target_pairs={{4,0},{8,4},{12,8},{16,12},{20,16},{24,20},{28,24},{5,1},{9,5},{13... | collective-permute-start | bytes 1474568 | tf_op jit(solution)/shard_map/ppermute | solution.py:30
  254.1 4.7 %collective-permute-start.10 = (f32[6,1,3,5,2,256]{5,1,4,3,2,0:T(1,128)S(1)}, f32[6,1,3,5,2,256]{5,1,4,3,2,0:T(1,128)S(1)}, u32[]{:S(2)}, u32[]{:S(2)}) collective-permute-start(f32[6,1,3,5,2,256]{5,1,4,3,2,0:T(1,128)S(1)} %get-tuple-element.72), channel_id=1, source_target_pairs={{0,1},{1,2},{2,3},{4,5},{5,6},{6,7},{8,9},{9,10},{10,11},{12,13},{... | collective-permute-start | bytes 552968 | tf_op jit(solution)/shard_map/ppermute | solution.py:28
  256.1 6.9 %collective-permute-start.11 = (f32[6,1,3,5,2,256]{5,1,4,3,2,0:T(1,128)S(1)}, f32[6,1,3,5,2,256]{5,1,4,3,2,0:T(1,128)S(1)}, u32[]{:S(2)}, u32[]{:S(2)}) collective-permute-start(f32[6,1,3,5,2,256]{5,1,4,3,2,0:T(1,128)S(1)} %get-tuple-element.73), channel_id=1, source_target_pairs={{1,0},{2,1},{3,2},{5,4},{6,5},{7,6},{9,8},{10,9},{11,10},{13,12},{... | collective-permute-start | bytes 552968 | tf_op jit(solution)/shard_map/ppermute | solution.py:30
  270.7 3.2 %copy-start.2 = (f32[6,18,3,5,2,256]{5,1,4,3,2,0:T(8,128)S(1)}, f32[6,18,3,5,2,256]{5,1,4,3,2,0:T(8,128)}, u32[]{:S(2)}) copy-start(f32[6,18,3,5,2,256]{5,1,4,3,2,0:T(8,128)} %scatter.14) | copy-start | bytes 9953284
  277.7 1.5 copy-start.3
  277.8 2.1 copy-start.4
  280.4 1.0 copy-start.6
  282.0 1.5 copy-start.5
  283.5 4.3 %copy-start.1 = (f32[32,32]{1,0:T(8,128)S(1)}, f32[32,32]{1,0:T(8,128)}, u32[]{:S(2)}) copy-start(f32[32,32]{1,0:T(8,128)} %param.19) | copy-start | bytes 12292
Sparse Core Ops, SparseCore 0:
  23.2 132.3 all-reduce.1
where the time goes:
time: 297 us; the launch traced here: 295 us
  waiting for transfers between devices  170 us (57%)
  local copies, waits for them, and re-layouts  38.5 us (13%)
  other arithmetic  32.1 us (11%)
  starting transfers between devices  31.7 us (11%)
  between operations  14.7 us (5%)
  matrix products  7.93 us (3%)
    psum x1, waiting for transfers between devices, on_device(): totals = lax.psum(partial_value, ('ax', 'rad'))  115 us
    ppermute x6, waiting for transfers between devices, extended(): lax.ppermute(tail, axis, [(i, (i + 1) % count) for i in range(ends)])  46.2 us
    ppermute x6, starting transfers between devices, extended(): lax.ppermute(tail, axis, [(i, (i + 1) % count) for i in range(ends)])  21.3 us
    scatter x3, local copies, waits for them, and re-layouts, on_device(): padded = padded.at[0, 1:-1].set(ghost)  14.8 us
    ppermute x6, starting transfers between devices, extended(): lax.ppermute(head, axis, [((i + 1) % count, i) for i in range(ends)])  10.3 us
    concatenate x3, other arithmetic, extended(): jnp.concatenate([lax.ppermute(tail, axis, [(i, (i + 1) % count) for i in...  9.55 us
    ppermute x6, waiting for transfers between devices, extended(): lax.ppermute(head, axis, [((i + 1) % count, i) for i in range(ends)])  8.53 us
    unnamed x40, local copies, waits for them, and re-layouts  7.62 us
  transfers between devices with their start and end apart: 13, of which 7 were waited for; matrix products, arithmetic and copies ran while one was open for 5% of the time, Pallas kernels for 0%

commit v1 on v0

v1 whole, which is shorter than its diff:
```python
import functools
import math

import jax
import jax.numpy as jnp
from jax import lax
from jax.experimental import pallas as pl
from jax.experimental.pallas import tpu as pltpu
from jax.sharding import PartitionSpec as P

NTH = 512
SAMPLE_MOMENTS = 7
HARM = 3
NMODE = 256
NRM = 32
NRD = 64
ITERS = 3
VARS = 5

OMEGA_STEP = 0.35
DAMPING = 0.25

MESH = pl.DeviceIdType.MESH
GROUP = VARS * 2 * 2
PLANES = HARM * GROUP
PAD = 8


def dot_nt(a, b):
    return lax.dot_general(
        a, b, (((1,), (1,)), ((), ())),
        precision=lax.Precision.HIGHEST, preferred_element_type=jnp.float32,
    )


def dot_nn(a, b):
    return lax.dot_general(
        a, b, (((1,), (0,)), ((), ())),
        precision=lax.Precision.HIGHEST, preferred_element_type=jnp.float32,
    )


def kernel(
    n_ax, n_rad, layers, rows,
    x_hbm, face, weights, cosine, sine, shapes, mach, step, invr, mode_r,
    out,
    T, part, a_recv, total, c_recv, b_recv, bound,
    load_sem, ax_send, ax_recv, rad_send, rad_recv, late_send, late_recv,
    a_send, a_sem, c_send, c_sem, b_send, b_sem, d_send, d_sem,
):
    ax = lax.axis_index("ax")
    rad = lax.axis_index("rad")
    share = PLANES // n_rad
    own = pl.ds(PAD, rows)
    peers_c = n_ax // 2 - 1
    top = layers + 1

    barrier = pltpu.get_barrier_semaphore()

    def greet(**where):
        pl.semaphore_signal(barrier, inc=1, device_id=where, device_id_type=MESH)

    pl.when(ax > 0)(lambda: greet(ax=ax - 1))
    pl.when(ax < n_ax - 1)(lambda: greet(ax=ax + 1))
    for d in range(1, n_rad):
        greet(rad=lax.rem(rad + d, n_rad))
    pl.when(ax >= 2)(lambda: greet(ax=lax.rem(ax, 2)))

    @pl.when(ax < 2)
    def _():
        for i in range(peers_c):
            greet(ax=ax + 2 * (i + 1))

    count = (
        jnp.where(ax > 0, 1, 0) + jnp.where(ax < n_ax - 1, 1, 0) + (n_rad - 1)
        + jnp.where(ax >= 2, 1, peers_c)
    )
    pl.semaphore_wait(barrier, count)

    def group(k):
        return pl.ds(k * GROUP, GROUP)

    def axial(t, k, side):
        source_layer = layers if side == 0 else 1
        if t == 0:
            src = x_hbm.at[source_layer - 1, group(k)]
        else:
            src = T.at[t, source_layer, group(k), own]
        return pltpu.make_async_remote_copy(
            src_ref=src,
            dst_ref=T.at[t, 0 if side == 0 else top, group(k), own],
            send_sem=ax_send.at[t, k, side],
            recv_sem=ax_recv.at[t, k, side],
            device_id={"ax": ax + 1 if side == 0 else ax - 1},
            device_id_type=MESH,
        )

    def radial(t, k, side, lo, hi, late=False):
        count_l = hi - lo
        first = rows - PAD if side == 0 else 0
        if t == 0:
            src = x_hbm.at[pl.ds(lo - 1, count_l), group(k), pl.ds(first, PAD)]
        else:
            src = T.at[t, pl.ds(lo, count_l), group(k), pl.ds(PAD + first, PAD)]
        send, recv = (late_send, late_recv) if late else (rad_send, rad_recv)
        return pltpu.make_async_remote_copy(
            src_ref=src,
            dst_ref=T.at[
                t, pl.ds(lo, count_l), group(k), pl.ds(0 if side == 0 else PAD + rows, PAD)
            ],
            send_sem=send.at[t, k, side],
            recv_sem=recv.at[t, k, side],
            device_id={"rad": rad + 1 if side == 0 else rad - 1},
            device_id_type=MESH,
        )

    can_send = {
        ("ax", 0): ax < n_ax - 1, ("ax", 1): ax > 0,
        ("rad", 0): rad < n_rad - 1, ("rad", 1): rad > 0,
    }
    can_recv = {
        ("ax", 0): ax > 0, ("ax", 1): ax < n_ax - 1,
        ("rad", 0): rad > 0, ("rad", 1): rad < n_rad - 1,
    }

    def axial_all(t, k, what):
        table = can_recv if what == "wait_recv" else can_send
        for side in (0, 1):
            pl.when(table["ax", side])(
                lambda side=side: getattr(axial(t, k, side), what)()
            )

    def radial_all(t, k, what):
        table = can_recv if what == "wait_recv" else can_send
        for side in (0, 1):
            if t == 0:
                pl.when(table["rad", side])(
                    lambda side=side: getattr(radial(0, k, side, 1, top), what)()
                )
            else:
                pl.when(table["rad", side] & (ax > 0))(
                    lambda side=side: getattr(radial(t, k, side, 1, top), what)()
                )
                pl.when(table["rad", side] & (ax == 0))(
                    lambda side=side: getattr(radial(t, k, side, t + 1, top), what)()
                )

    def radial_late(t, k, what):
        table = can_recv if what == "wait_recv" else can_send
        for side in (0, 1):
            pl.when(table["rad", side])(
                lambda side=side: getattr(radial(t, k, side, 1, t + 1, True), what)()
            )

    for k in range(HARM):
        axial_all(0, k, "start")
        radial_all(0, k, "start")
    load = pltpu.make_async_copy(
        x_hbm, T.at[0, pl.ds(1, layers), :, own], load_sem
    )
    load.start()

    zero_rows = jnp.zeros((PAD, 128), jnp.float32)

    @pl.when(ax == n_ax - 1)
    def _():
        @pl.loop(0, PLANES)
        def _(q):
            for t in range(ITERS):
                T[t, top, q, own, :] = jnp.zeros((rows, 128), jnp.float32)

    for edge, start in ((rad == 0, 0), (rad == n_rad - 1, PAD + rows)):
        @pl.when(edge)
        def _(start=start):
            @pl.loop(0, PLANES)
            def _(q):
                for t in range(ITERS):
                    for l in range(1, top):
                        T[t, l, q, pl.ds(start, PAD), :] = zero_rows

    slots = face.shape[1]
    for v in range(VARS):
        spectra = dot_nt(weights[...], face[v])
        half = HARM * NRM
        y0, y1 = spectra[:half], spectra[half:]
        real = dot_nn(y0, cosine[...]) + dot_nn(y1, sine[...])
        imag = dot_nn(y1, cosine[...]) - dot_nn(y0, sine[...])
        for c, value in ((0, real), (1, imag)):
            for k in range(HARM):
                for sh in range(2):
                    part[k * GROUP + v * 4 + c * 2 + sh] = value[
                        k * NRM:(k + 1) * NRM, sh * 128:(sh + 1) * 128
                    ]

    def scatter(d):
        peer = lax.rem(rad + d, n_rad)
        return pltpu.make_async_remote_copy(
            src_ref=part.at[pl.ds(peer * share, share)],
            dst_ref=a_recv.at[d - 1],
            send_sem=a_send.at[d - 1],
            recv_sem=a_sem.at[d - 1],
            device_id={"rad": peer},
            device_id_type=MESH,
        )

    for d in range(1, n_rad):
        scatter(d).start()
    for d in range(1, n_rad):
        scatter(d).wait_recv()

    @pl.loop(0, share)
    def _(q):
        acc = part[rad * share + q]
        for d in range(n_rad - 1):
            acc = acc + a_recv[d, q]
        total[0, q] = acc

    def to_front():
        return pltpu.make_async_remote_copy(
            src_ref=total.at[0],
            dst_ref=c_recv.at[ax // 2 - 1],
            send_sem=c_send,
            recv_sem=c_sem.at[ax // 2 - 1],
            device_id={"ax": lax.rem(ax, 2)},
            device_id_type=MESH,
        )

    def to_inlet():
        return pltpu.make_async_remote_copy(
            src_ref=total.at[1],
            dst_ref=b_recv,
            send_sem=b_send,
            recv_sem=b_sem,
            device_id={"ax": 0},
            device_id_type=MESH,
        )

    def hand_out(d):
        peer = lax.rem(rad + d, n_rad)
        return pltpu.make_async_remote_copy(
            src_ref=bound.at[peer],
            dst_ref=T.at[0, 0, pl.ds(rad * share, share), own],
            send_sem=d_send.at[d - 1],
            recv_sem=d_sem.at[d - 1],
            device_id={"rad": peer},
            device_id_type=MESH,
        )

    def gather_front():
        for i in range(peers_c):
            pltpu.make_async_copy(c_recv.at[i], c_recv.at[i], c_sem.at[i]).wait()

        @pl.loop(0, share)
        def _(q):
            acc = total[0, q]
            for i in range(peers_c):
                acc = acc + c_recv[i, q]
            total[1, q] = acc

    pl.when(ax >= 2)(lambda: to_front().start())
    load.wait()

    def update(t, k, lo, hi):
        omega = OMEGA_STEP * (k + 1).astype(jnp.float32)

        def layer_body(i, carry):
            l = lo + i // 2
            sh = lax.rem(i, 2)
            for h in range(rows // 8):
                r0 = PAD + 8 * h
                here = pl.ds(8 * h, 8)
                m = mach[l - 1, here, :]
                dt = step[l - 1, here, :]
                ir = invr[here, :]
                mr = mode_r[sh, here, :]
                base = k * GROUP + sh

                def get(v, c, dl=0, dr=0):
                    return T[t, l + dl, base + v * 4 + c * 2, pl.ds(r0 + dr, 8), :]

                centre = [[get(v, c) for c in (0, 1)] for v in range(VARS)]

                def rot(v, c):
                    return -centre[v][1] if c == 0 else centre[v][0]

                def diff(v, c):
                    up, dn = get(v, c, 1), get(v, c, -1)
                    rt, lf = get(v, c, 0, 1), get(v, c, 0, -1)
                    along = (up - dn) * 0.5
                    across = (rt - lf) * 0.5
                    return along, across, (up + dn) + (rt + lf) - 4.0 * centre[v][c]

                for c in (0, 1):
                    d = [diff(v, c) for v in range(VARS)]
                    source = d[1][0] + d[2][1] + centre[2][c] * ir + rot(3, c) * mr
                    extra = [source, d[4][0], d[4][1], rot(4, c) * mr, source]
                    for v in range(VARS):
                        residual = omega * rot(v, c) + m * d[v][0] + extra[v]
                        value = centre[v][c] - dt * (residual - DAMPING * d[v][2])
                        q = base + v * 4 + c * 2
                        if t == ITERS - 1:
                            out[l - 1, q, here, :] = value
                        else:
                            T[t + 1, l, q, pl.ds(r0, 8), :] = value
            return carry

        lax.fori_loop(0, 2 * (hi - lo), layer_body, 0)

    def early(t):
        @pl.loop(0, HARM)
        def _(k):
            radial_all(t, k, "wait_recv")
            axial_all(t, k, "wait_recv")
            update(t, k, jnp.where(ax == 0, t + 2, 1), top)
            if t < ITERS - 1:
                axial_up_down(t + 1, k)
                radial_all(t + 1, k, "start")

    def axial_up_down(t, k):
        axial_all(t, k, "start")

    def late(t):
        @pl.loop(0, HARM)
        def _(k):
            if t > 0:
                radial_late(t, k, "wait_recv")
            update(t, k, 1, t + 2)
            if t < ITERS - 1:
                radial_late(t + 1, k, "start")

    early(0)

    @pl.when(ax < 2)
    def _():
        gather_front()

    pl.when(ax == 1)(lambda: to_inlet().start())
    early(1)

    @pl.when(ax == 0)
    def _():
        to_inlet_wait = pltpu.make_async_copy(b_recv, b_recv, b_sem)
        to_inlet_wait.wait()

        @pl.loop(0, share)
        def _(q):
            value = dot_nn(shapes[...], total[1, q] + b_recv[q])
            for r in range(n_rad):
                bound[r, q] = value[r * rows:(r + 1) * rows]

        for d in range(1, n_rad):
            hand_out(d).start()

        @pl.loop(0, share)
        def _(q):
            T[0, 0, rad * share + q, own, :] = bound[rad, q]

        for d in range(1, n_rad):
            src = lax.rem(rad + n_rad - d, n_rad)
            place = T.at[0, 0, pl.ds(src * share, share), own]
            pltpu.make_async_copy(place, place, d_sem.at[d - 1]).wait()

        @pl.loop(0, PLANES)
        def _(q):
            value = T[0, 0, q, own, :]
            for t in range(1, ITERS):
                T[t, 0, q, own, :] = value

        late(0)
        late(1)

    early(2)
    pl.when(ax == 0)(lambda: late(2))

    for t in range(ITERS):
        @pl.loop(0, HARM)
        def _(k):
            axial_all(t, k, "wait_send")
            radial_all(t, k, "wait_send")
            if t > 0:
                pl.when(ax == 0)(lambda: radial_late(t, k, "wait_send"))
    for d in range(1, n_rad):
        scatter(d).wait_send()
    pl.when(ax >= 2)(lambda: to_front().wait_send())
    pl.when(ax == 1)(lambda: to_inlet().wait_send())

    @pl.when(ax == 0)
    def _():
        for d in range(1, n_rad):
            hand_out(d).wait_send()


def on_device(
    n_ax, n_rad,
    face_data, face_station, face_counts, mode_slots, radial_proj, radial_modes,
    duct_field, mean_mach, pseudo_step,
):
    layers, rows = duct_field.shape[:2]
    slots = face_station.shape[0]
    valid = jnp.arange(slots) < face_counts[0]
    orders = mode_slots - NMODE // 2
    frequency_order = jnp.arange(1, HARM + 1)
    moments = jnp.arange(SAMPLE_MOMENTS)
    turns = (frequency_order[:, None] * moments[None, :] % SAMPLE_MOMENTS).astype(
        jnp.float32
    ) * (2.0 * math.pi / SAMPLE_MOMENTS)
    twiddle = jnp.stack([jnp.cos(turns), -jnp.sin(turns)], axis=0) * (2.0 / SAMPLE_MOMENTS)
    width = face_data.shape[3]
    weights = (
        twiddle[:, :, None, :, None] * radial_proj[None, None, :, None, :]
    ).reshape(2 * HARM * NRM, SAMPLE_MOMENTS * width)
    face = jnp.transpose(face_data, (2, 0, 1, 3)).reshape(VARS, slots, SAMPLE_MOMENTS * width)
    phase = jnp.mod(face_station[:, None] * orders[None, :], NTH).astype(jnp.float32) * (
        2.0 * math.pi / NTH
    )
    cosine = jnp.where(valid[:, None], jnp.cos(phase), 0.0)
    sine = jnp.where(valid[:, None], jnp.sin(phase), 0.0)

    radial_start = lax.axis_index("rad") * rows
    global_rows = (radial_start + jnp.arange(rows)).astype(jnp.float32)
    inv_radius = 1.0 / (NRD + global_rows + 0.5)
    modes = orders.astype(jnp.float32).reshape(2, 1, 128)
    invr = jnp.broadcast_to(inv_radius[:, None], (rows, 128))
    mode_r = modes * inv_radius[None, :, None]
    mach = jnp.broadcast_to(mean_mach[:, :, None], (layers, rows, 128))
    step = jnp.broadcast_to(pseudo_step[:, :, None], (layers, rows, 128))
    x = jnp.transpose(
        duct_field.reshape(layers, rows, PLANES // 2, 2, 128), (0, 2, 3, 1, 4)
    ).reshape(layers, PLANES, rows, 128)

    share = PLANES // n_rad
    vmem = pl.BlockSpec(memory_space=pltpu.VMEM)
    dma = pltpu.SemaphoreType.DMA
    out = pl.pallas_call(
        functools.partial(kernel, n_ax, n_rad, layers, rows),
        out_shape=jax.ShapeDtypeStruct((layers, PLANES, rows, 128), jnp.float32),
        in_specs=[pl.BlockSpec(memory_space=pl.ANY)] + [vmem] * 9,
        out_specs=vmem,
        scratch_shapes=[
            pltpu.VMEM((ITERS, layers + 2, PLANES, rows + 2 * PAD, 128), jnp.float32),
            pltpu.VMEM((PLANES, NRM, 128), jnp.float32),
            pltpu.VMEM((n_rad - 1, share, NRM, 128), jnp.float32),
            pltpu.VMEM((2, share, NRM, 128), jnp.float32),
            pltpu.VMEM((n_ax // 2 - 1, share, NRM, 128), jnp.float32),
            pltpu.VMEM((share, NRM, 128), jnp.float32),
            pltpu.VMEM((n_rad, share, rows, 128), jnp.float32),
            dma,
            dma((ITERS, HARM, 2)), dma((ITERS, HARM, 2)),
            dma((ITERS, HARM, 2)), dma((ITERS, HARM, 2)),
            dma((ITERS, HARM, 2)), dma((ITERS, HARM, 2)),
            dma((n_rad - 1,)), dma((n_rad - 1,)),
            dma, dma((n_ax // 2 - 1,)),
            dma, dma,
            dma((n_rad - 1,)), dma((n_rad - 1,)),
        ],
        compiler_params=pltpu.CompilerParams(
            collective_id=0, has_side_effects=True, vmem_limit_bytes=60 * 1024 * 1024
        ),
    )(x, face, weights, cosine, sine, radial_modes, mach, step, invr, mode_r)
    return jnp.transpose(
        out.reshape(layers, PLANES // 2, 2, rows, 128), (0, 3, 1, 2, 4)
    ).reshape(duct_field.shape)


def solution(mesh):
    in_specs = (
        P("ax", None, None, "rad"),
        P("ax"),
        P("ax"),
        P(),
        P(None, "rad"),
        P(),
        P("ax", "rad", None, None, None, None),
        P("ax", "rad"),
        P("ax", "rad"),
    )
    out_specs = P("ax", "rad", None, None, None, None)
    return jax.shard_map(
        functools.partial(on_device, mesh.shape["ax"], mesh.shape["rad"]),
        mesh=mesh, in_specs=in_specs, out_specs=out_specs, check_vma=False,
    )
```

time: 297 us -> 102 us (0.34)
  waiting for transfers between devices: 170 us -> 0 us
  Pallas kernels: 0 us -> 77.8 us
  starting transfers between devices: 31.7 us -> 0 us
  other arithmetic: 32.1 us -> 3.59 us
  local copies, waits for them, and re-layouts: 38.5 us -> 19 us
  between operations: 14.7 us -> 0.72 us
  matrix products: 7.93 us -> 0 us
    psum x1 -> x0, waiting for transfers between devices: 115 us -> none  [on_device(): totals = lax.psum(partial_value, ('ax', 'rad'))]
    pallas_call x0 -> x1, Pallas kernels: none -> 77.8 us  [on_device(): pl.pallas_call(functools.partial(kernel, n_ax, n_rad, layers, rows), out_...]
    ppermute x12 -> x0, waiting for transfers between devices: 54.7 us -> none  [the longest x6 46.2 us: extended(): lax.ppermute(tail, axis, [(i, (i + 1) % count) for i in range(ends)])]
    ppermute x12 -> x0, starting transfers between devices: 31.7 us -> none  [the longest x6 21.3 us: extended(): lax.ppermute(tail, axis, [(i, (i + 1) % count) for i in range(ends)])]
    scatter x3 -> x0, local copies, waits for them, and re-layouts: 14.8 us -> none  [on_device(): padded = padded.at[0, 1:-1].set(ghost)]
    reshape x0 -> x4, local copies, waits for them, and re-layouts: none -> 9.65 us  [the longest x2 5.06 us: on_device(): duct_field.reshape(layers, rows, PLANES // 2, 2, 128)]
    concatenate x3 -> x0, other arithmetic: 9.55 us -> none  [extended(): jnp.concatenate([lax.ppermute(tail, axis, [(i, (i + 1) % count) for i in...]
    slice x4 -> x0, other arithmetic: 8.16 us -> none  [the longest x1 6.62 us: advance(): centre = padded[1:-1, 1:-1]]
  transfers between devices with their start and end apart: 13 -> 0, of which waited for: 7 -> 0; matrix products, arithmetic and copies ran while one was open for 5% -> 0% of each run, Pallas kernels for 0% -> 0%
where the time goes in v1:
time: 102 us; the launch traced here: 101 us
  Pallas kernels  77.8 us (76%)
  local copies, waits for them, and re-layouts  19 us (19%)
  other arithmetic  3.59 us (4%)
    pallas_call x1, Pallas kernels, on_device(): pl.pallas_call(functools.partial(kernel, n_ax, n_rad, layers, rows), out_...  77.8 us
    reshape x2, local copies, waits for them, and re-layouts, on_device(): duct_field.reshape(layers, rows, PLANES // 2, 2, 128)  5.06 us
    reshape x1, local copies, waits for them, and re-layouts, on_device(): return jnp.transpose(out.reshape(layers, PLANES // 2, 2, rows, 128), (0,...  3.52 us
    transpose x1, local copies, waits for them, and re-layouts, on_device(): jnp.transpose(out.reshape(layers, PLANES // 2, 2, rows, 128), (0, 3, 1, 2...  2.56 us
    unnamed x4, local copies, waits for them, and re-layouts  2.5 us

profile of v1, /device:TPU:1, one launch (start us, length us, event | category | flops | bytes accessed | tf_op | source)
XLA Modules:
  0.0 101.1 jit_solution(10735939942251788779)
XLA Ops:
  0.0 0.0 copy-start
  0.7 0.7 convert_bitcast_fusion
  1.4 0.1 fusion.8
  1.5 0.7 broadcast_in_dim.26.invr
  2.2 0.7 broadcast_multiply_fusion.1.mode_r
  2.8 1.4 %copy.17.shapes = f32[64,32]{1,0:T(8,128)} copy(f32[64,32]{0,1:T(8,128)} %param.14) | data formatting | bytes 16384 | tf_op args[5]
  4.2 1.4 %broadcast_in_dim.24.mach = f32[4,16,128]{2,1,0:T(8,128)} broadcast(f32[4,16]{1,0:T(4,128)} %param.16), dimensions={0,1} | broadcast | bytes 33024 | tf_op jit(solution)/shard_map/broadcast_in_dim | solution.py:425
  5.6 1.4 %broadcast_in_dim.25.step = f32[4,16,128]{2,1,0:T(8,128)} broadcast(f32[4,16]{1,0:T(4,128)} %param.17), dimensions={0,1} | broadcast | bytes 33024 | tf_op jit(solution)/shard_map/broadcast_in_dim | solution.py:426
  7.0 2.0 %sine_select_fusion = (f32[128,256]{1,0:T(8,128)}, f32[128,256]{1,0:T(8,128)}) fusion(s32[256]{0:T(256)S(1)} %get-tuple-element.8, s32[128]{0:T(128)} %param.10, pred[128]{0:T(512)(128)(4,1)S(1)} %iota_compare_fusion), kind=kLoop, calls=%fused_computation.9 | loop fusion | flops 524288 | bytes 263808 | tf_op jit(solution)/shard_map/jit(_where)/select_n | solution.py:417
  8.9 1.1 %copy.15 = f32[128,7,5,32]{0,3,1,2:T(8,128)S(1)} copy(f32[128,7,5,32]{0,3,2,1:T(8,128)} %param.9) | data formatting | bytes 1146880 | tf_op args[0]
  10.0 1.1 %copy.16.face = f32[5,128,224]{2,1,0:T(8,128)} copy(f32[5,128,224]{1,2,0:T(8,128)S(1)} %bitcast.15) | data formatting | bytes 1146880 | tf_op jit(solution)/shard_map/reshape | solution.py:412
  11.1 0.0 copy-done
  11.1 0.1 broadcast_multiply_fusion
  11.2 0.9 mul.127.weights
  12.1 3.5 %reshape.150 = f32[4,16,30,2,128]{4,3,2,1,0:T(2,128)S(1)} reshape(f32[4,16,3,5,2,256]{5,4,3,2,1,0:T(2,128)} %param.15) | data formatting | bytes 3932160 | tf_op jit(solution)/shard_map/reshape | solution.py:428
  15.7 1.5 %copy.14 = f32[4,16,30,2,128]{4,1,3,2,0:T(8,128)} copy(f32[4,16,30,2,128]{4,3,2,1,0:T(2,128)S(1)} %reshape.150) | data formatting | bytes 3932160 | tf_op jit(solution)/shard_map/reshape | solution.py:428
  17.2 77.8 %shard_map.91 = f32[4,60,16,128]{3,2,1,0:T(8,128)} custom-call(f32[4,60,16,128]{3,2,1,0:T(8,128)} %bitcast.13, f32[5,128,224]{2,1,0:T(8,128)} %copy.16.face, f32[192,224]{1,0:T(8,128)} %mul.127.weights, f32[128,256]{1,0:T(8,128)} %get-tuple-element.6.cosine, f32[128,256]{1,0:T(8,128)} %get-tuple-element.5.sine, f32[64,32]{1,0:T(8,128)} %copy.17.shapes, ...), custom_call_target="tpu_custom_call" | custom-call | tf_op jit(solution)/shard_map/pallas_call | solution.py:434
  95.0 2.6 %copy.18 = f32[4,16,30,2,128]{4,3,2,1,0:T(2,128)S(1)} copy(f32[4,16,30,2,128]{4,1,3,2,0:T(8,128)} %bitcast.14) | data formatting | bytes 3932160 | tf_op jit(solution)/shard_map/transpose | solution.py:460
  97.6 3.5 %reshape.154 = f32[4,16,3,5,2,256]{5,4,3,2,1,0:T(2,128)} reshape(f32[4,16,30,2,128]{4,3,2,1,0:T(2,128)S(1)} %copy.18) | data formatting | bytes 3932160 | tf_op jit(solution)/shard_map/reshape | solution.py:462
  (4 shorter events, 0.0 us)
Async XLA Ops:
  0.0 11.1 %copy-start = (f32[32,32]{1,0:T(8,128)S(1)}, f32[32,32]{1,0:T(8,128)}, u32[]{:S(2)}) copy-start(f32[32,32]{1,0:T(8,128)} %param.13) | copy-start | bytes 12292

commit v2 on v1

v2 whole, which is shorter than its diff:
```python
import functools
import math

import jax
import jax.numpy as jnp
from jax import lax
from jax.experimental import pallas as pl
from jax.experimental.pallas import tpu as pltpu
from jax.sharding import PartitionSpec as P

NTH = 512
SAMPLE_MOMENTS = 7
HARM = 3
NMODE = 256
NRM = 32
NRD = 64
ITERS = 3
VARS = 5

OMEGA_STEP = 0.35
DAMPING = 0.25

MESH = pl.DeviceIdType.MESH
GROUP = VARS * 2
PLANES = HARM * GROUP
PAD = 8
HALF = 128
SLOTS = 32
STEPS = (
    (0, 0), (0, 1), (1, 0), (2, 0), (0, 2), (1, 1),
    (3, 0), (2, 1), (1, 2), (3, 1), (2, 2), (3, 2),
)


def dot_nn(a, b):
    return lax.dot_general(
        a, b, (((1,), (0,)), ((), ())),
        precision=lax.Precision.HIGHEST, preferred_element_type=jnp.float32,
    )


def kernel(
    n_ax, n_rad, layers, rows,
    x_hbm, face, weights, cosine, sine, shapes, coef_in, invr, mode_r,
    out,
    T, coef, part, a_recv, total, y_recv, merged, c_recv, bound, ghost,
    load_sem, out_sem, coef_load, coef_send, coef_recv,
    in_send, in_recv, back_send, back_recv,
    z_send, z_recv, rad_send, rad_recv, late_send, late_recv,
    a_send, a_sem, y_send, y_sem, c_send, c_sem, d_send, d_sem,
):
    ax = lax.axis_index("ax")
    rad = lax.axis_index("rad")
    side_y = lax.rem(ax, 2)
    pair = ax // 2
    mate = ax + 1 - 2 * side_y
    pairs = n_ax // 2
    deep = 2 * layers
    top = deep + 1
    own = pl.ds(PAD, rows)
    share = 2 * SLOTS // n_rad
    half_share = share // 2
    mine = 1 + side_y * layers
    theirs = 1 + (1 - side_y) * layers
    my_lanes = pl.ds(pl.multiple_of(side_y * HALF, HALF), HALF)
    their_lanes = pl.ds(pl.multiple_of((1 - side_y) * HALF, HALF), HALF)
    front = pair == 0
    per_half = n_rad // 2
    half_of = rad // per_half

    barrier = pltpu.get_barrier_semaphore()

    def greet(**where):
        pl.semaphore_signal(barrier, inc=1, device_id=where, device_id_type=MESH)

    greet(ax=mate)
    for d in range(1, n_rad):
        greet(rad=lax.rem(rad + d, n_rad))

    @pl.when(front)
    def _():
        for i in range(1, pairs):
            greet(ax=ax + 2 * i)
        for d in range(1, n_rad):
            pl.semaphore_signal(
                barrier, inc=1,
                device_id=(mate, lax.rem(rad + d, n_rad)), device_id_type=MESH,
            )

    @pl.when(pair > 0)
    def _():
        greet(ax=side_y)

    @pl.when(pair > 1)
    def _():
        greet(ax=ax - 2)

    @pl.when((pair > 0) & (pair < pairs - 1))
    def _():
        greet(ax=ax + 2)

    count = (
        1 + (n_rad - 1)
        + jnp.where(front, pairs - 1 + n_rad - 1, 1)
        + jnp.where(pair > 1, 1, 0)
        + jnp.where((pair > 0) & (pair < pairs - 1), 1, 0)
    )
    pl.semaphore_wait(barrier, count)

    def group(k):
        return pl.ds(k * GROUP, GROUP)

    def remote(src, dst, send, recv, **where):
        return pltpu.make_async_remote_copy(
            src_ref=src, dst_ref=dst, send_sem=send, recv_sem=recv,
            device_id=where, device_id_type=MESH,
        )

    def arrived(ref, sem):
        pltpu.make_async_copy(ref, ref, sem).wait()

    def fetch(k):
        return remote(
            x_hbm.at[:, group(k), :, their_lanes],
            T.at[0, pl.ds(mine, layers), group(k), own],
            in_send.at[k], in_recv.at[k], ax=mate,
        )

    def fetched(k):
        arrived(T.at[0, pl.ds(theirs, layers), group(k), own], in_recv.at[k])

    def give_back(k):
        return remote(
            T.at[ITERS, pl.ds(theirs, layers), group(k), own],
            out.at[:, group(k), :, my_lanes],
            back_send.at[k], back_recv.at[k], ax=mate,
        )

    def given(k):
        arrived(out.at[:, group(k), :, their_lanes], back_recv.at[k])

    def along_z(t, k, side):
        return remote(
            T.at[t, deep if side == 0 else 1, group(k), own],
            T.at[t, 0 if side == 0 else top, group(k), own],
            z_send.at[t, k, side], z_recv.at[t, k, side],
            ax=ax + 2 if side == 0 else ax - 2,
        )

    def radial(t, k, side, lo, count_l, late=False):
        first = rows - PAD if side == 0 else 0
        send, recv = (late_send, late_recv) if late else (rad_send, rad_recv)
        return remote(
            T.at[t, pl.ds(lo, count_l), group(k), pl.ds(PAD + first, PAD)],
            T.at[
                t, pl.ds(lo, count_l), group(k), pl.ds(0 if side == 0 else PAD + rows, PAD)
            ],
            send.at[t, k, side], recv.at[t, k, side],
            rad=rad + 1 if side == 0 else rad - 1,
        )

    can_send = {
        ("z", 0): pair < pairs - 1, ("z", 1): pair > 0,
        ("rad", 0): rad < n_rad - 1, ("rad", 1): rad > 0,
    }
    can_recv = {
        ("z", 0): pair > 0, ("z", 1): pair < pairs - 1,
        ("rad", 0): rad > 0, ("rad", 1): rad < n_rad - 1,
    }

    def z_all(t, k, what):
        table = can_recv if what == "wait_recv" else can_send
        for side in (0, 1):
            pl.when(table["z", side])(
                lambda side=side: getattr(along_z(t, k, side), what)()
            )

    def radial_all(t, k, what):
        table = can_recv if what == "wait_recv" else can_send
        for side in (0, 1):
            pl.when(table["rad", side] & ((pair > 0) | (t == 0)))(
                lambda side=side: getattr(radial(t, k, side, 1, deep), what)()
            )
            for s in range(1, ITERS):
                pl.when(table["rad", side] & front & (t == s))(
                    lambda side=side, s=s: getattr(radial(s, k, side, s + 1, deep - s), what)()
                )

    def radial_late(t, k, what):
        table = can_recv if what == "wait_recv" else can_send
        for side in (0, 1):
            for s in range(1, ITERS):
                pl.when(table["rad", side] & (t == s))(
                    lambda side=side, s=s: getattr(radial(s, k, side, 1, s, True), what)()
                )

    def give_coef():
        return remote(coef_in, coef.at[:, pl.ds(mine, layers)], coef_send, coef_recv, ax=mate)

    fetch(0).start()
    give_coef().start()
    for k in range(1, HARM):
        fetch(k).start()
    load = pltpu.make_async_copy(
        x_hbm.at[:, :, :, my_lanes], T.at[0, pl.ds(mine, layers), :, own], load_sem
    )
    load.start()
    keep_coef = pltpu.make_async_copy(coef_in, coef.at[:, pl.ds(mine, layers)], coef_load)
    keep_coef.start()

    zero_rows = jnp.zeros((PAD, 128), jnp.float32)

    @pl.when(pair == pairs - 1)
    def _():
        @pl.loop(0, PLANES)
        def _(q):
            for t in range(ITERS):
                T[t, top, q, own, :] = jnp.zeros((rows, 128), jnp.float32)

    for edge, start in ((rad == 0, 0), (rad == n_rad - 1, PAD + rows)):
        @pl.when(edge)
        def _(start=start):
            @pl.loop(0, PLANES)
            def _(q):
                for t in range(ITERS):
                    for l in range(1, top):
                        T[t, l, q, pl.ds(start, PAD), :] = zero_rows

    for sh in range(2):
        for q in range(PLANES, SLOTS):
            part[sh * SLOTS + q] = jnp.zeros((NRM, HALF), jnp.float32)
    for v in range(VARS):
        spectra = dot_nn(
            weights[...], jnp.concatenate([face[t, v] for t in range(SAMPLE_MOMENTS)], axis=0)
        )
        half = HARM * NRM
        y0, y1 = spectra[:half], spectra[half:]
        real = dot_nn(y0, cosine[...]) + dot_nn(y1, sine[...])
        imag = dot_nn(y1, cosine[...]) - dot_nn(y0, sine[...])
        for c, value in ((0, real), (1, imag)):
            for k in range(HARM):
                for sh in range(2):
                    part[sh * SLOTS + k * GROUP + v * 2 + c] = value[
                        k * NRM:(k + 1) * NRM, sh * HALF:(sh + 1) * HALF
                    ]

    def scatter(d):
        peer = lax.rem(rad + d, n_rad)
        return remote(
            part.at[pl.ds(peer * share, share)], a_recv.at[d - 1],
            a_send.at[d - 1], a_sem.at[d - 1], rad=peer,
        )

    for d in range(1, n_rad):
        scatter(d).start()

    load.wait()
    keep_coef.wait()

    def keep(kk):
        return pltpu.make_async_copy(
            T.at[ITERS, pl.ds(mine, layers), group(kk), own],
            out.at[:, group(kk), :, my_lanes],
            out_sem.at[kk],
        )

    def to_mate():
        return remote(
            total.at[pl.ds((1 - side_y) * half_share, half_share)], y_recv,
            y_send, y_sem, ax=mate,
        )

    def to_front():
        return remote(merged.at[0], c_recv.at[pair - 1], c_send, c_sem.at[pair - 1], ax=side_y)

    inside = half_of == side_y
    place = lax.rem(rad, per_half)

    def hand_out(r):
        return pltpu.make_async_remote_copy(
            src_ref=bound.at[r],
            dst_ref=ghost.at[pl.ds(place * share + side_y * half_share, half_share)],
            send_sem=d_send.at[r],
            recv_sem=d_sem.at[place * 2 + side_y],
            device_id=(half_of, r),
            device_id_type=MESH,
        )

    def hand_out_all(what):
        for r in range(n_rad):
            pl.when(jnp.logical_not(inside & (rad == r)))(
                lambda r=r: getattr(hand_out(r), what)()
            )

    def sum_rad():
        for d in range(1, n_rad):
            scatter(d).wait_recv()

        @pl.loop(0, share)
        def _(q):
            acc = part[rad * share + q]
            for d in range(n_rad - 1):
                acc = acc + a_recv[d, q]
            total[q] = acc

        to_mate().start()

    def sum_pair():
        arrived(y_recv, y_sem)

        @pl.loop(0, half_share)
        def _(q):
            merged[0, q] = total[side_y * half_share + q] + y_recv[q]

        pl.when(pair > 0)(lambda: to_front().start())

    def inlet():
        for i in range(pairs - 1):
            arrived(c_recv.at[i], c_sem.at[i])

        @pl.loop(0, half_share)
        def _(q):
            acc = merged[0, q]
            for i in range(pairs - 1):
                acc = acc + c_recv[i, q]
            value = dot_nn(shapes[...], acc)
            for r in range(n_rad):
                bound[r, q] = value[r * rows:(r + 1) * rows]

        hand_out_all("start")

        @pl.when(inside)
        def _():
            @pl.loop(0, half_share)
            def _(q):
                ghost[place * share + side_y * half_share + q] = bound[rad, q]

    def inlet_arrived():
        for i in range(per_half):
            for sy in range(2):
                pl.when(jnp.logical_not(inside & (place == i) & (side_y == sy)))(
                    lambda i=i, sy=sy: arrived(
                        ghost.at[pl.ds(i * share + sy * half_share, half_share)],
                        d_sem.at[i * 2 + sy],
                    )
                )

        @pl.loop(0, PLANES)
        def _(q):
            value = ghost[q]
            for t in range(ITERS):
                T[t, 0, q, own, :] = value

    def update(t, k, lo, hi):
        omega = OMEGA_STEP * (k + 1).astype(jnp.float32)
        base = k * GROUP

        def layer_body(l, carry):
            for h in range(rows // 8):
                r0 = PAD + 8 * h
                here = pl.ds(8 * h, 8)
                m = coef[0, l, here, :]
                dt = coef[1, l, here, :]
                ir = invr[here, :]
                mr = mode_r[side_y, here, :]

                def get(v, c, dl=0, dr=0):
                    return T[t, l + dl, base + v * 2 + c, pl.ds(r0 + dr, 8), :]

                centre = [[get(v, c) for c in (0, 1)] for v in range(VARS)]

                def rot(v, c):
                    return -centre[v][1] if c == 0 else centre[v][0]

                def diff(v, c):
                    up, dn = get(v, c, 1), get(v, c, -1)
                    rt, lf = get(v, c, 0, 1), get(v, c, 0, -1)
                    along = (up - dn) * 0.5
                    across = (rt - lf) * 0.5
                    return along, across, (up + dn) + (rt + lf) - 4.0 * centre[v][c]

                for c in (0, 1):
                    d = [diff(v, c) for v in range(VARS)]
                    source = d[1][0] + d[2][1] + centre[2][c] * ir + rot(3, c) * mr
                    extra = [source, d[4][0], d[4][1], rot(4, c) * mr, source]
                    for v in range(VARS):
                        residual = omega * rot(v, c) + m * d[v][0] + extra[v]
                        value = centre[v][c] - dt * (residual - DAMPING * d[v][2])
                        T[t + 1, l, base + v * 2 + c, pl.ds(r0, 8), :] = value
            return carry

        lax.fori_loop(lo, hi, layer_body, 0)

    def pick(i, values):
        chosen = 0
        for j, value in enumerate(values):
            if value:
                chosen = chosen + jnp.where(i == j, value, 0)
        return chosen

    @pl.loop(0, len(STEPS))
    def _(i):
        t = pick(i, [s[0] for s in STEPS])
        k = pick(i, [s[1] for s in STEPS])

        @pl.when(t == 0)
        def _():
            fetched(k)

        @pl.when(i == 0)
        def _():
            arrived(coef.at[:, pl.ds(theirs, layers)], coef_recv)

        @pl.when(t > 0)
        def _():
            radial_all(t - 1, k, "wait_recv")
            z_all(t - 1, k, "wait_recv")
            update(t - 1, k, jnp.where(front, t + 1, 1), top)

        @pl.when(t < ITERS)
        def _():
            z_all(t, k, "start")
            radial_all(t, k, "start")

        @pl.when((t == ITERS) & (ax != 1))
        def _():
            give_back(k).start()

        @pl.when((t == ITERS) & (ax != 0))
        def _():
            keep(k).start()

        pl.when(i == 1)(sum_rad)
        pl.when(i == 4)(sum_pair)
        pl.when((i == 8) & front)(inlet)

    @pl.when(front)
    def _():
        inlet_arrived()

        @pl.loop(0, ITERS * HARM)
        def _(i):
            t = i // HARM
            k = lax.rem(i, HARM)
            radial_late(t, k, "wait_recv")
            update(t, k, 1, t + 2)
            radial_late(t + 1, k, "start")

            @pl.when((t == ITERS - 1) & (ax == 1))
            def _():
                give_back(k).start()

            @pl.when((t == ITERS - 1) & (ax == 0))
            def _():
                keep(k).start()

    give_coef().wait_send()

    @pl.loop(0, HARM)
    def _(k):
        fetch(k).wait_send()
        given(k)
        give_back(k).wait_send()
        keep(k).wait()

    @pl.loop(0, ITERS * HARM)
    def _(i):
        t = i // HARM
        k = lax.rem(i, HARM)
        z_all(t, k, "wait_send")
        radial_all(t, k, "wait_send")
        pl.when(front)(lambda: radial_late(t, k, "wait_send"))

    for d in range(1, n_rad):
        scatter(d).wait_send()
    to_mate().wait_send()
    pl.when(pair > 0)(lambda: to_front().wait_send())
    pl.when(front)(lambda: hand_out_all("wait_send"))


def on_device(
    n_ax, n_rad,
    face_data, face_station, face_counts, mode_slots, radial_proj, radial_modes,
    duct_field, mean_mach, pseudo_step,
):
    layers, rows = duct_field.shape[:2]
    slots = face_station.shape[0]
    valid = jnp.arange(slots) < face_counts[0]
    orders = mode_slots - NMODE // 2
    frequency_order = jnp.arange(1, HARM + 1)
    moments = jnp.arange(SAMPLE_MOMENTS)
    turns = (frequency_order[:, None] * moments[None, :] % SAMPLE_MOMENTS).astype(
        jnp.float32
    ) * (2.0 * math.pi / SAMPLE_MOMENTS)
    twiddle = jnp.stack([jnp.cos(turns), -jnp.sin(turns)], axis=0) * (2.0 / SAMPLE_MOMENTS)
    width = face_data.shape[3]
    weights = (
        twiddle[:, :, None, :, None] * radial_proj[None, None, :, None, :]
    ).reshape(2 * HARM * NRM, SAMPLE_MOMENTS * width)
    face = jnp.transpose(face_data, (1, 2, 3, 0))
    phase = jnp.mod(face_station[:, None] * orders[None, :], NTH).astype(jnp.float32) * (
        2.0 * math.pi / NTH
    )
    cosine = jnp.where(valid[:, None], jnp.cos(phase), 0.0)
    sine = jnp.where(valid[:, None], jnp.sin(phase), 0.0)

    radial_start = lax.axis_index("rad") * rows
    global_rows = (radial_start + jnp.arange(rows)).astype(jnp.float32)
    inv_radius = 1.0 / (NRD + global_rows + 0.5)
    modes = orders.astype(jnp.float32).reshape(2, 1, 128)
    invr = jnp.broadcast_to(inv_radius[:, None], (rows, 128))
    mode_r = modes * inv_radius[None, :, None]
    coef = jnp.broadcast_to(
        jnp.stack([mean_mach, pseudo_step])[..., None], (2, layers, rows, HALF)
    )
    x = jnp.transpose(duct_field.reshape(layers, rows, PLANES, NMODE), (0, 2, 1, 3))

    share = 2 * SLOTS // n_rad
    half_share = share // 2
    pairs = n_ax // 2
    deep = 2 * layers
    vmem = pl.BlockSpec(memory_space=pltpu.VMEM)
    anywhere = pl.BlockSpec(memory_space=pl.ANY)
    dma = pltpu.SemaphoreType.DMA
    per_side = dma((ITERS, HARM, 2))
    out = pl.pallas_call(
        functools.partial(kernel, n_ax, n_rad, layers, rows),
        out_shape=jax.ShapeDtypeStruct((layers, PLANES, rows, NMODE), jnp.float32),
        in_specs=[anywhere] + [vmem] * 8,
        out_specs=anywhere,
        scratch_shapes=[
            pltpu.VMEM((ITERS + 1, deep + 2, PLANES, rows + 2 * PAD, HALF), jnp.float32),
            pltpu.VMEM((2, deep + 2, rows, HALF), jnp.float32),
            pltpu.VMEM((2 * SLOTS, NRM, HALF), jnp.float32),
            pltpu.VMEM((n_rad - 1, share, NRM, HALF), jnp.float32),
            pltpu.VMEM((share, NRM, HALF), jnp.float32),
            pltpu.VMEM((half_share, NRM, HALF), jnp.float32),
            pltpu.VMEM((1, half_share, NRM, HALF), jnp.float32),
            pltpu.VMEM((pairs - 1, half_share, NRM, HALF), jnp.float32),
            pltpu.VMEM((n_rad, half_share, rows, HALF), jnp.float32),
            pltpu.VMEM((SLOTS, rows, HALF), jnp.float32),
            dma, dma((HARM,)), dma, dma, dma,
            dma((HARM,)), dma((HARM,)), dma((HARM,)), dma((HARM,)),
            per_side, per_side, per_side, per_side, per_side, per_side,
            dma((n_rad - 1,)), dma((n_rad - 1,)),
            dma, dma, dma, dma((pairs - 1,)),
            dma((n_rad,)), dma((n_rad,)),
        ],
        compiler_params=pltpu.CompilerParams(
            collective_id=0, has_side_effects=True, vmem_limit_bytes=60 * 1024 * 1024
        ),
    )(x, face, weights, cosine, sine, radial_modes, coef, invr, mode_r)
    return jnp.transpose(out, (0, 2, 1, 3)).reshape(duct_field.shape)


def solution(mesh):
    in_specs = (
        P("ax", None, None, "rad"),
        P("ax"),
        P("ax"),
        P(),
        P(None, "rad"),
        P(),
        P("ax", "rad", None, None, None, None),
        P("ax", "rad"),
        P("ax", "rad"),
    )
    out_specs = P("ax", "rad", None, None, None, None)
    return jax.shard_map(
        functools.partial(on_device, mesh.shape["ax"], mesh.shape["rad"]),
        mesh=mesh, in_specs=in_specs, out_specs=out_specs, check_vma=False,
    )
```

time: 102 us -> 107 us (1.049)
  Pallas kernels: 77.8 us -> 91.4 us
  local copies, waits for them, and re-layouts: 19 us -> 9.55 us
  other arithmetic: 3.59 us -> 5 us
    pallas_call x1, Pallas kernels: 77.8 us -> 91.4 us  [on_device(): pl.pallas_call(functools.partial(kernel, n_ax, n_rad, layers, rows), out_...]
    reshape x4 -> x1, local copies, waits for them, and re-layouts: 9.65 us -> 4.33 us  [on_device(): return jnp.transpose(out, (0, 2, 1, 3)).reshape(duct_field.shape)]
    transpose x1 -> x0, local copies, waits for them, and re-layouts: 2.56 us -> none  [on_device(): jnp.transpose(out.reshape(layers, PLANES // 2, 2, rows, 128), (0, 3, 1, 2...]
    broadcast_in_dim x2 -> x1, local copies, waits for them, and re-layouts: 2.71 us -> 0.7 us  [on_device(): jnp.broadcast_to(jnp.stack([mean_mach, pseudo_step])[..., None], (2, laye...]
where the time goes in v2:
time: 107 us
  Pallas kernels  91.4 us (85%)
  local copies, waits for them, and re-layouts  9.55 us (9%)
  other arithmetic  5 us (5%)
    pallas_call x1, Pallas kernels, on_device(): pl.pallas_call(functools.partial(kernel, n_ax, n_rad, layers, rows), out_...  91.4 us
    reshape x1, local copies, waits for them, and re-layouts, on_device(): return jnp.transpose(out, (0, 2, 1, 3)).reshape(duct_field.shape)  4.33 us
    unnamed x4, local copies, waits for them, and re-layouts  2.95 us

profile of v2, /device:TPU:1, one launch (start us, length us, event | category | flops | bytes accessed | tf_op | source)
XLA Modules:
  0.0 106.8 jit_solution(10283862338377639245)
XLA Ops:
  0.0 0.0 copy-start
  0.8 0.7 convert_bitcast_fusion
  1.5 0.1 fusion.8
  1.7 0.7 pad_maximum_fusion
  2.4 0.7 broadcast_in_dim.23.invr
  3.0 0.7 broadcast_multiply_fusion.1.mode_r
  3.7 1.4 %copy.14.shapes = f32[64,32]{1,0:T(8,128)} copy(f32[64,32]{0,1:T(8,128)} %param.14) | data formatting | bytes 16384 | tf_op args[5]
  5.1 0.7 broadcast_in_dim.22.coef_in
  5.8 2.0 %sine_select_fusion = (f32[128,256]{1,0:T(8,128)}, f32[128,256]{1,0:T(8,128)}) fusion(s32[256]{0:T(256)S(1)} %get-tuple-element.8, s32[128]{0:T(128)} %param.10, pred[128]{0:T(512)(128)(4,1)S(1)} %iota_compare_fusion), kind=kLoop, calls=%fused_computation.9 | loop fusion | flops 524288 | bytes 263808 | tf_op jit(solution)/shard_map/jit(_where)/select_n | solution.py:505
  7.8 0.8 broadcast_multiply_fusion
  8.6 0.9 mul.127.weights
  9.5 0.0 copy-done
  9.5 1.5 %copy.13 = f32[4,16,3,5,2,256]{5,1,4,3,2,0:T(8,128)} copy(f32[4,16,3,5,2,256]{5,4,3,2,1,0:T(2,128)S(1)} %copy-done) | data formatting | bytes 3932160 | tf_op args[6]
  11.0 91.4 %shard_map.91 = f32[4,30,16,256]{3,2,1,0:T(8,128)} custom-call(f32[4,30,16,256]{3,2,1,0:T(8,128)} %bitcast.14, f32[7,5,32,128]{3,2,1,0:T(8,128)} %bitcast.15, f32[192,224]{1,0:T(8,128)} %mul.127.weights, f32[128,256]{1,0:T(8,128)} %get-tuple-element.6.cosine, f32[128,256]{1,0:T(8,128)} %get-tuple-element.5.sine, f32[64,32]{1,0:T(8,128)} %copy.14.shapes, ...), custom_call_target="tpu_custom_call" | custom-call | tf_op jit(solution)/shard_map/pallas_call | solution.py:526
  102.4 4.3 %copy.15 = f32[4,16,3,5,2,256]{5,4,3,2,1,0:T(2,128)} copy(f32[4,16,3,5,2,256]{5,1,4,3,2,0:T(8,128)} %bitcast.13) | data formatting | bytes 3932160 | tf_op jit(solution)/shard_map/reshape | solution.py:553
  (4 shorter events, 0.0 us)
Async XLA Ops:
  0.0 9.5 %copy-start = (f32[4,16,3,5,2,256]{5,4,3,2,1,0:T(2,128)S(1)}, f32[4,16,3,5,2,256]{5,4,3,2,1,0:T(2,128)}, u32[]{:S(2)}) copy-start(f32[4,16,3,5,2,256]{5,4,3,2,1,0:T(2,128)} %param.15) | copy-start | bytes 5898244

commit v3 on v2

--- a/solution.py
+++ b/solution.py
@@ -43,10 +43,10 @@
     n_ax, n_rad, layers, rows,
     x_hbm, face, weights, cosine, sine, shapes, coef_in, invr, mode_r,
     out,
-    T, coef, part, a_recv, total, y_recv, merged, c_recv, bound, ghost,
+    T, D, land, coef, part, a_recv, total, y_recv, merged, c_recv, bound, ghost,
     load_sem, out_sem, coef_load, coef_send, coef_recv,
     in_send, in_recv, back_send, back_recv,
-    z_send, z_recv, rad_send, rad_recv, late_send, late_recv,
+    z_send, z_recv, rad_send, rad_recv, late_send, late_recv, put_sem,
     a_send, a_sem, y_send, y_sem, c_send, c_sem, d_send, d_sem,
 ):
     ax = lax.axis_index("ax")
@@ -65,8 +65,6 @@
     my_lanes = pl.ds(pl.multiple_of(side_y * HALF, HALF), HALF)
     their_lanes = pl.ds(pl.multiple_of((1 - side_y) * HALF, HALF), HALF)
     front = pair == 0
-    per_half = n_rad // 2
-    half_of = rad // per_half
 
     barrier = pltpu.get_barrier_semaphore()
 
@@ -132,12 +130,12 @@
     def give_back(k):
         return remote(
             T.at[ITERS, pl.ds(theirs, layers), group(k), own],
-            out.at[:, group(k), :, my_lanes],
+            land.at[:, group(k)],
             back_send.at[k], back_recv.at[k], ax=mate,
         )
 
     def given(k):
-        arrived(out.at[:, group(k), :, their_lanes], back_recv.at[k])
+        arrived(land.at[:, group(k)], back_recv.at[k])
 
     def along_z(t, k, side):
         return remote(
@@ -147,15 +145,22 @@
             ax=ax + 2 if side == 0 else ax - 2,
         )
 
-    def radial(t, k, side, lo, count_l, late=False):
+    def radial(t, k, side):
         first = rows - PAD if side == 0 else 0
-        send, recv = (late_send, late_recv) if late else (rad_send, rad_recv)
+        layers_all = pl.ds(1, deep)
         return remote(
-            T.at[t, pl.ds(lo, count_l), group(k), pl.ds(PAD + first, PAD)],
-            T.at[
-                t, pl.ds(lo, count_l), group(k), pl.ds(0 if side == 0 else PAD + rows, PAD)
-            ],
-            send.at[t, k, side], recv.at[t, k, side],
+            T.at[t, layers_all, group(k), pl.ds(PAD + first, PAD)],
+            T.at[t, layers_all, group(k), pl.ds(0 if side == 0 else PAD + rows, PAD)],
+            rad_send.at[t, k, side], rad_recv.at[t, k, side],
+            rad=rad + 1 if side == 0 else rad - 1,
+        )
+
+    def radial_inlet(t, hs, side):
+        first = rows - PAD if side == 0 else 0
+        return remote(
+            D.at[hs, t, pl.ds(1, t), :, pl.ds(PAD + first, PAD)],
+            D.at[hs, t, pl.ds(1, t), :, pl.ds(0 if side == 0 else PAD + rows, PAD)],
+            late_send.at[t, hs, side], late_recv.at[t, hs, side],
             rad=rad + 1 if side == 0 else rad - 1,
         )
 
@@ -178,20 +183,16 @@
     def radial_all(t, k, what):
         table = can_recv if what == "wait_recv" else can_send
         for side in (0, 1):
-            pl.when(table["rad", side] & ((pair > 0) | (t == 0)))(
-                lambda side=side: getattr(radial(t, k, side, 1, deep), what)()
+            pl.when(table["rad", side])(
+                lambda side=side: getattr(radial(t, k, side), what)()
             )
-            for s in range(1, ITERS):
-                pl.when(table["rad", side] & front & (t == s))(
-                    lambda side=side, s=s: getattr(radial(s, k, side, s + 1, deep - s), what)()
-                )
-
-    def radial_late(t, k, what):
+
+    def radial_inlet_all(t, what):
         table = can_recv if what == "wait_recv" else can_send
-        for side in (0, 1):
-            for s in range(1, ITERS):
-                pl.when(table["rad", side] & (t == s))(
-                    lambda side=side, s=s: getattr(radial(s, k, side, 1, s, True), what)()
+        for hs in (0, 1):
+            for side in (0, 1):
+                pl.when(table["rad", side])(
+                    lambda hs=hs, side=side: getattr(radial_inlet(t, hs, side), what)()
                 )
 
     def give_coef():
@@ -217,6 +218,25 @@
             for t in range(ITERS):
                 T[t, top, q, own, :] = jnp.zeros((rows, 128), jnp.float32)
 
+    @pl.when(front)
+    def _():
+        @pl.loop(0, PLANES)
+        def _(q):
+            for t in range(ITERS):
+                T[t, 0, q, own, :] = jnp.zeros((rows, 128), jnp.float32)
+
+    @pl.when(ax == 0)
+    def _():
+        @pl.loop(0, PLANES)
+        def _(q):
+            for hs in range(2):
+                for t in range(ITERS):
+                    for l in (t + 1, t + 2):
+                        D[hs, t, l, q] = jnp.zeros((rows + 2 * PAD, 128), jnp.float32)
+                    for l in range(1, t + 1):
+                        D[hs, t, l, q, pl.ds(0, PAD), :] = zero_rows
+                        D[hs, t, l, q, pl.ds(PAD + rows, PAD), :] = zero_rows
+
     for edge, start in ((rad == 0, 0), (rad == n_rad - 1, PAD + rows)):
         @pl.when(edge)
         def _(start=start):
@@ -273,22 +293,19 @@
     def to_front():
         return remote(merged.at[0], c_recv.at[pair - 1], c_send, c_sem.at[pair - 1], ax=side_y)
 
-    inside = half_of == side_y
-    place = lax.rem(rad, per_half)
-
     def hand_out(r):
         return pltpu.make_async_remote_copy(
             src_ref=bound.at[r],
-            dst_ref=ghost.at[pl.ds(place * share + side_y * half_share, half_share)],
+            dst_ref=ghost.at[pl.ds(rad * share + side_y * half_share, half_share)],
             send_sem=d_send.at[r],
-            recv_sem=d_sem.at[place * 2 + side_y],
-            device_id=(half_of, r),
+            recv_sem=d_sem.at[rad * 2 + side_y],
+            device_id=(0, r),
             device_id_type=MESH,
         )
 
     def hand_out_all(what):
         for r in range(n_rad):
-            pl.when(jnp.logical_not(inside & (rad == r)))(
+            pl.when(jnp.logical_not((ax == 0) & (rad == r)))(
                 lambda r=r: getattr(hand_out(r), what)()
             )
 
@@ -329,16 +346,16 @@
 
         hand_out_all("start")
 
-        @pl.when(inside)
+        @pl.when(ax == 0)
         def _():
             @pl.loop(0, half_share)
             def _(q):
-                ghost[place * share + side_y * half_share + q] = bound[rad, q]
+                ghost[rad * share + q] = bound[rad, q]
 
     def inlet_arrived():
-        for i in range(per_half):
+        for i in range(n_rad):
             for sy in range(2):
-                pl.when(jnp.logical_not(inside & (place == i) & (side_y == sy)))(
+                pl.when(jnp.logical_not((rad == i) & (sy == 0)))(
                     lambda i=i, sy=sy: arrived(
                         ghost.at[pl.ds(i * share + sy * half_share, half_share)],
                         d_sem.at[i * 2 + sy],
@@ -347,11 +364,12 @@
 
         @pl.loop(0, PLANES)
         def _(q):
-            value = ghost[q]
-            for t in range(ITERS):
-                T[t, 0, q, own, :] = value
-
-    def update(t, k, lo, hi):
+            for hs in range(2):
+                value = ghost[hs * SLOTS + q]
+                for t in range(ITERS):
+                    D[hs, t, 0, q, own, :] = value
+
+    def update(buf, where, sh, t, k, lo, hi):
         omega = OMEGA_STEP * (k + 1).astype(jnp.float32)
         base = k * GROUP
 
@@ -362,10 +380,10 @@
                 m = coef[0, l, here, :]
                 dt = coef[1, l, here, :]
                 ir = invr[here, :]
-                mr = mode_r[side_y, here, :]
+                mr = mode_r[sh, here, :]
 
                 def get(v, c, dl=0, dr=0):
-                    return T[t, l + dl, base + v * 2 + c, pl.ds(r0 + dr, 8), :]
+                    return buf[(*where, t, l + dl, base + v * 2 + c, pl.ds(r0 + dr, 8), slice(None))]
 
                 centre = [[get(v, c) for c in (0, 1)] for v in range(VARS)]
 
@@ -386,7 +404,7 @@
                     for v in range(VARS):
                         residual = omega * rot(v, c) + m * d[v][0] + extra[v]
                         value = centre[v][c] - dt * (residual - DAMPING * d[v][2])
-                        T[t + 1, l, base + v * 2 + c, pl.ds(r0, 8), :] = value
+                        buf[(*where, t + 1, l, base + v * 2 + c, pl.ds(r0, 8), slice(None))] = value
             return carry
 
         lax.fori_loop(lo, hi, layer_body, 0)
@@ -415,14 +433,14 @@
         def _():
             radial_all(t - 1, k, "wait_recv")
             z_all(t - 1, k, "wait_recv")
-            update(t - 1, k, jnp.where(front, t + 1, 1), top)
+            update(T, (), side_y, t - 1, k, 1, top)
 
         @pl.when(t < ITERS)
         def _():
             z_all(t, k, "start")
             radial_all(t, k, "start")
 
-        @pl.when((t == ITERS) & (ax != 1))
+        @pl.when(t == ITERS)
         def _():
             give_back(k).start()
 
@@ -434,33 +452,57 @@
         pl.when(i == 4)(sum_pair)
         pl.when((i == 8) & front)(inlet)
 
-    @pl.when(front)
+    def put(k):
+        return pltpu.make_async_copy(
+            land.at[:, group(k)], out.at[:, group(k), :, their_lanes], put_sem.at[k]
+        )
+
+    @pl.when(ax == 0)
     def _():
         inlet_arrived()
-
-        @pl.loop(0, ITERS * HARM)
-        def _(i):
-            t = i // HARM
-            k = lax.rem(i, HARM)
-            radial_late(t, k, "wait_recv")
-            update(t, k, 1, t + 2)
-            radial_late(t + 1, k, "start")
-
-            @pl.when((t == ITERS - 1) & (ax == 1))
-            def _():
-                give_back(k).start()
-
-            @pl.when((t == ITERS - 1) & (ax == 0))
-            def _():
-                keep(k).start()
+        for t in range(ITERS):
+            if t > 0:
+                radial_inlet_all(t, "wait_recv")
+
+            @pl.loop(0, 2 * HARM)
+            def _(i, t=t):
+                hs = i // HARM
+                update(D, (hs,), hs, t, lax.rem(i, HARM), 1, t + 2)
+
+            if t < ITERS - 1:
+                radial_inlet_all(t + 1, "start")
+
+        @pl.loop(0, HARM)
+        def _(k):
+            @pl.loop(0, GROUP)
+            def _(j):
+                q = k * GROUP + j
+                for l in range(1, ITERS + 1):
+                    T[ITERS, l, q, own, :] = T[ITERS, l, q, own, :] + D[0, ITERS, l, q, own, :]
+
+            keep(k).start()
+
+    @pl.loop(0, HARM)
+    def _(k):
+        given(k)
+
+        @pl.when(ax == 0)
+        def _():
+            @pl.loop(0, GROUP)
+            def _(j):
+                q = k * GROUP + j
+                for l in range(1, ITERS + 1):
+                    land[l - 1, q] = land[l - 1, q] + D[1, ITERS, l, q, own, :]
+
+        put(k).start()
 
     give_coef().wait_send()
 
     @pl.loop(0, HARM)
     def _(k):
         fetch(k).wait_send()
-        given(k)
         give_back(k).wait_send()
+        put(k).wait()
         keep(k).wait()
 
     @pl.loop(0, ITERS * HARM)
@@ -469,13 +511,17 @@
         k = lax.rem(i, HARM)
         z_all(t, k, "wait_send")
         radial_all(t, k, "wait_send")
-        pl.when(front)(lambda: radial_late(t, k, "wait_send"))
 
     for d in range(1, n_rad):
         scatter(d).wait_send()
     to_mate().wait_send()
     pl.when(pair > 0)(lambda: to_front().wait_send())
     pl.when(front)(lambda: hand_out_all("wait_send"))
+
+    @pl.when(ax == 0)
+    def _():
+        for t in range(1, ITERS):
+            radial_inlet_all(t, "wait_send")
 
 
 def on_device(
@@ -530,6 +576,8 @@
         out_specs=anywhere,
         scratch_shapes=[
             pltpu.VMEM((ITERS + 1, deep + 2, PLANES, rows + 2 * PAD, HALF), jnp.float32),
+            pltpu.VMEM((2, ITERS + 1, ITERS + 2, PLANES, rows + 2 * PAD, HALF), jnp.float32),
+            pltpu.VMEM((layers, PLANES, rows, HALF), jnp.float32),
             pltpu.VMEM((2, deep + 2, rows, HALF), jnp.float32),
             pltpu.VMEM((2 * SLOTS, NRM, HALF), jnp.float32),
             pltpu.VMEM((n_rad - 1, share, NRM, HALF), jnp.float32),
@@ -538,13 +586,13 @@
             pltpu.VMEM((1, half_share, NRM, HALF), jnp.float32),
             pltpu.VMEM((pairs - 1, half_share, NRM, HALF), jnp.float32),
             pltpu.VMEM((n_rad, half_share, rows, HALF), jnp.float32),
-            pltpu.VMEM((SLOTS, rows, HALF), jnp.float32),
+            pltpu.VMEM((2 * SLOTS, rows, HALF), jnp.float32),
             dma, dma((HARM,)), dma, dma, dma,
             dma((HARM,)), dma((HARM,)), dma((HARM,)), dma((HARM,)),
-            per_side, per_side, per_side, per_side, per_side, per_side,
+            per_side, per_side, per_side, per_side, per_side, per_side, dma((HARM,)),
             dma((n_rad - 1,)), dma((n_rad - 1,)),
             dma, dma, dma, dma((pairs - 1,)),
-            dma((n_rad,)), dma((n_rad,)),
+            dma((n_rad,)), dma((2 * n_rad,)),
         ],
         compiler_params=pltpu.CompilerParams(
             collective_id=0, has_side_effects=True, vmem_limit_bytes=60 * 1024 * 1024

time: 107 us -> 99.4 us (0.929)
  Pallas kernels: 91.4 us -> 83.6 us
    pallas_call x1, Pallas kernels: 91.4 us -> 83.6 us  [on_device(): pl.pallas_call(functools.partial(kernel, n_ax, n_rad, layers, rows), out_...]
where the time goes in v3:
time: 99.4 us; the launch traced here: 99 us
  Pallas kernels  83.6 us (84%)
  local copies, waits for them, and re-layouts  9.55 us (10%)
  other arithmetic  5 us (5%)
    pallas_call x1, Pallas kernels, on_device(): pl.pallas_call(functools.partial(kernel, n_ax, n_rad, layers, rows), out_...  83.6 us
    reshape x1, local copies, waits for them, and re-layouts, on_device(): return jnp.transpose(out, (0, 2, 1, 3)).reshape(duct_field.shape)  4.33 us
    unnamed x4, local copies, waits for them, and re-layouts  2.95 us

profile of v3, /device:TPU:1, one launch (start us, length us, event | category | flops | bytes accessed | tf_op | source)
XLA Modules:
  0.0 99.0 jit_solution(12157625772971498144)
XLA Ops:
  0.0 0.0 copy-start
  0.8 0.7 convert_bitcast_fusion
  1.5 0.1 fusion.8
  1.7 0.7 pad_maximum_fusion
  2.4 0.7 broadcast_in_dim.23.invr
  3.0 0.7 broadcast_multiply_fusion.1.mode_r
  3.7 1.4 %copy.14.shapes = f32[64,32]{1,0:T(8,128)} copy(f32[64,32]{0,1:T(8,128)} %param.14) | data formatting | bytes 16384 | tf_op args[5]
  5.1 0.7 broadcast_in_dim.22.coef_in
  5.8 2.0 %sine_select_fusion = (f32[128,256]{1,0:T(8,128)}, f32[128,256]{1,0:T(8,128)}) fusion(s32[256]{0:T(256)S(1)} %get-tuple-element.8, s32[128]{0:T(128)} %param.10, pred[128]{0:T(512)(128)(4,1)S(1)} %iota_compare_fusion), kind=kLoop, calls=%fused_computation.9 | loop fusion | flops 524288 | bytes 263808 | tf_op jit(solution)/shard_map/jit(_where)/select_n | solution.py:551
  7.8 0.8 broadcast_multiply_fusion
  8.6 0.9 mul.127.weights
  9.5 0.0 copy-done
  9.5 1.5 %copy.13 = f32[4,16,3,5,2,256]{5,1,4,3,2,0:T(8,128)} copy(f32[4,16,3,5,2,256]{5,4,3,2,1,0:T(2,128)S(1)} %copy-done) | data formatting | bytes 3932160 | tf_op args[6]
  11.0 83.6 %shard_map.91 = f32[4,30,16,256]{3,2,1,0:T(8,128)} custom-call(f32[4,30,16,256]{3,2,1,0:T(8,128)} %bitcast.14, f32[7,5,32,128]{3,2,1,0:T(8,128)} %bitcast.15, f32[192,224]{1,0:T(8,128)} %mul.127.weights, f32[128,256]{1,0:T(8,128)} %get-tuple-element.6.cosine, f32[128,256]{1,0:T(8,128)} %get-tuple-element.5.sine, f32[64,32]{1,0:T(8,128)} %copy.14.shapes, ...), custom_call_target="tpu_custom_call" | custom-call | tf_op jit(solution)/shard_map/pallas_call | solution.py:572
  94.6 4.3 %copy.15 = f32[4,16,3,5,2,256]{5,4,3,2,1,0:T(2,128)} copy(f32[4,16,3,5,2,256]{5,1,4,3,2,0:T(8,128)} %bitcast.13) | data formatting | bytes 3932160 | tf_op jit(solution)/shard_map/reshape | solution.py:601
  (4 shorter events, 0.0 us)
Async XLA Ops:
  0.0 9.5 %copy-start = (f32[4,16,3,5,2,256]{5,4,3,2,1,0:T(2,128)S(1)}, f32[4,16,3,5,2,256]{5,4,3,2,1,0:T(2,128)}, u32[]{:S(2)}) copy-start(f32[4,16,3,5,2,256]{5,4,3,2,1,0:T(2,128)} %param.15) | copy-start | bytes 5898244
